TPU v7x, 32 devices: a whole 2x2x4 slice. The times are simulated.
32 devices in a mesh: dp: 8 (over z, y), tensor: 4 (over x, core).
Axes of the slice: x: 2, y: 2, z: 4, core: 2. Of those that a mesh axis runs over, the one named last changes fastest.
Arguments:
- tokens: bfloat16 [8, 4, 512, 768], P(None, 'tensor', 'dp'), may hold values from -6 to 6
- cotangent: bfloat16 [8, 2048, 768], P('dp', 'tensor'), may hold values from -6 to 6
- lengths: int32 [8], replicated, may hold values from 1 to 2048, 12288 in all
- dealt_to: int32 [8], replicated, may hold values from 0 to 7, each once
- adapter_id: int32 [8], replicated, may hold values from 0 to 7
- norm_gain: bfloat16 [768], replicated, may hold values from 0.25 to 1.75
- w_zx: bfloat16 [768, 2, 1536], P('dp', None, 'tensor'), may hold values from -0.21875 to 0.21875
- w_dt: bfloat16 [768, 24], P('dp', 'tensor'), may hold values from -0.21875 to 0.21875
- w_bc: bfloat16 [768, 256], P('dp'), may hold values from -0.21875 to 0.21875
- x_kernel: float32 [4, 1536], P(None, 'tensor'), may hold values from -3 to 3
- x_offset: float32 [1536], P('tensor'), may hold values from -0.5 to 0.5
- bc_kernel: float32 [4, 256], replicated, may hold values from -3 to 3
- bc_offset: float32 [256], replicated, may hold values from -0.5 to 0.5
- dt_bias: float32 [24], P('tensor'), may hold values from -6.9 to -2.3
- a_log: float32 [24], P('tensor'), may hold values from 0 to 2.77
- d_skip: float32 [24], P('tensor'), may hold values from 0.5 to 1.5
- out_gain: bfloat16 [1536], P('tensor'), may hold values from 0.25 to 1.75
- w_out: bfloat16 [1536, 768], P('tensor', 'dp'), may hold values from -0.15625 to 0.15625
- inlet_down: bfloat16 [8, 768, 16], replicated, may hold values from -0.21875 to 0.21875
- inlet_up: bfloat16 [8, 16, 2, 1536], P(None, None, None, 'tensor'), may hold values from -1.5 to 1.5
- outlet_down: bfloat16 [8, 1536, 16], replicated, may hold values from -0.15625 to 0.15625
- outlet_up: bfloat16 [8, 16, 768], replicated, may hold values from -1.5 to 1.5
Outputs:
- output: bfloat16 [8, 2048, 768], P('dp', 'tensor')
- token_grads: bfloat16 [8, 4, 512, 768], P(None, 'tensor', 'dp')
- inlet_dgrad: float32 [8, 768, 16], replicated
- inlet_ugrad: float32 [8, 16, 2, 1536], P(None, None, None, 'tensor')
- outlet_dgrad: float32 [8, 1536, 16], replicated
- outlet_ugrad: float32 [8, 16, 768], replicated
Inputs may be any that keep to these rules, and one draw needn't show every extreme that they name: `lengths`: the longest sequence has exactly 2048 positions. `dealt_to`: every group is named by exactly one sequence.
All inputs are finite; a program needn't handle non-finite values.
Results may differ from a plain program's by a relative error of at most 0.0085.
Values may be sent and summed in bfloat16 or wider, within the bound.
A program may use at most 128 MiB of HBM per device.

v0:
```python
from functools import partial

import jax
import jax.numpy as jnp
from jax import lax
from jax.sharding import PartitionSpec as P

INNER = 1536
SPAN = 256
ADAPTERS = 8


EPSILON = 1e-05
HIGHEST = lax.Precision.HIGHEST


def causal_conv(values, kernel, offsets):
    kernel_width = kernel.shape[0]
    length = values.shape[0]
    padded = jnp.pad(values, ((kernel_width - 1, 0), (0, 0)))
    running = jnp.zeros_like(values) + offsets[None, :]
    for offset in range(kernel_width):
        running = running + kernel[offset][None, :] * padded[offset : offset + length]
    return running


def state_mixer(heads_x, step_size, decay_rates, input_b, input_c):
    length, head_count, head_dim = heads_x.shape
    blocks = length // SPAN
    state_dim = input_b.shape[1]
    block_x = heads_x.reshape(blocks, SPAN, head_count, head_dim)
    block_dt = step_size.reshape(blocks, SPAN, head_count)
    block_b = input_b.reshape(blocks, SPAN, state_dim)
    block_c = input_c.reshape(blocks, SPAN, state_dim)
    causal = jnp.arange(SPAN)[:, None] >= jnp.arange(SPAN)[None, :]
    within = jnp.einsum(
        "ts,csh->cth",
        causal.astype(jnp.float32),
        block_dt * decay_rates[None, None, :],
        precision=HIGHEST,
    )
    scores = jnp.einsum("ctn,csn->cts", block_c, block_b, precision=HIGHEST)
    causal_full = causal[None, :, :, None]
    spread = within[:, :, None, :] - within[:, None, :, :]
    mixing = jnp.where(causal_full, jnp.exp(jnp.where(causal_full, spread, 0.0)), 0.0)
    weights = scores[:, :, :, None] * mixing * block_dt[:, None, :, :]
    inside = jnp.einsum("ctsh,cshp->cthp", weights, block_x, precision=HIGHEST)
    span_total = within[:, -1, :]
    tail_weight = jnp.exp(span_total[:, None, :] - within) * block_dt
    fresh_state = jnp.einsum("cth,cthp,ctn->chpn", tail_weight, block_x, block_b, precision=HIGHEST)
    span_ids = jnp.arange(blocks)
    through = jnp.einsum(
        "dc,ch->dh",
        (span_ids[:, None] >= span_ids[None, :]).astype(jnp.float32),
        span_total,
        precision=HIGHEST,
    )
    before = through - span_total
    earlier = (span_ids[:, None] > span_ids[None, :])[:, :, None]
    passing = jnp.where(
        earlier, jnp.exp(jnp.where(earlier, before[:, None, :] - through[None, :, :], 0.0)), 0.0
    )
    state_in = jnp.einsum("dch,chpn->dhpn", passing, fresh_state, precision=HIGHEST)
    carried = (
        jnp.einsum("ctn,chpn->cthp", block_c, state_in, precision=HIGHEST)
        * jnp.exp(within)[:, :, :, None]
    )
    return (inside + carried).reshape(length, head_count, head_dim)


def mixer_part(weights_local, p_zx, p_bc, p_dt):
    x_kernel, x_offset, bc_kernel, bc_offset, dt_bias, a_log, d_skip = weights_local
    length = p_zx.shape[0]
    inner_local = p_zx.shape[2]
    head_count = p_dt.shape[1]
    state_dim = p_bc.shape[1] // 2
    inner_x = jax.nn.silu(causal_conv(p_zx[:, 1, :], x_kernel, x_offset))
    mixed_bc = jax.nn.silu(causal_conv(p_bc, bc_kernel, bc_offset))
    step_size = jax.nn.softplus(p_dt + dt_bias)
    heads_x = inner_x.reshape(length, head_count, inner_local // head_count)
    mixed = state_mixer(
        heads_x, step_size, -jnp.exp(a_log), mixed_bc[:, :state_dim], mixed_bc[:, state_dim:]
    )
    mixed = mixed + d_skip[None, :, None] * heads_x
    return mixed.reshape(length, inner_local) * jax.nn.silu(p_zx[:, 0, :])


def shards(
    tokens,
    cotangent,
    lengths,
    dealt_to,
    adapter_id,
    norm_gain,
    w_zx,
    w_dt,
    w_bc,
    x_kernel,
    x_offset,
    bc_kernel,
    bc_offset,
    dt_bias,
    a_log,
    d_skip,
    out_gain,
    w_out,
    inlet_down,
    inlet_up,
    outlet_down,
    outlet_up,
):
    model_dim = tokens.shape[3]
    inner_local = w_zx.shape[2]
    full_zx, full_dt, full_bc, full_out = (
        lax.all_gather(w_zx, "dp", axis=0, tiled=True),
        lax.all_gather(w_dt, "dp", axis=0, tiled=True),
        lax.all_gather(w_bc, "dp", axis=0, tiled=True),
        lax.all_gather(w_out, "dp", axis=1, tiled=True),
    )
    seq_count = dealt_to.shape[0]
    slot_ids = jnp.arange(seq_count, dtype=jnp.int32)
    placed = (dealt_to[None, :] == slot_ids[:, None]).astype(jnp.int32)
    seq_of = jnp.sum(placed * slot_ids[None, :], axis=1)
    picked = jnp.take(tokens, seq_of, axis=0)
    arrived = lax.all_to_all(picked, "dp", split_axis=0, concat_axis=2, tiled=True)
    tok_rows = arrived.reshape(-1, model_dim)
    tok_dev = tok_rows.shape[0]
    group_id = lax.axis_index("dp")
    own_seq = jnp.take(seq_of, group_id)
    chosen = (jnp.arange(ADAPTERS, dtype=jnp.int32) == jnp.take(adapter_id, own_seq)).astype(
        jnp.float32
    )
    positions = lax.axis_index("tensor") * tok_dev + jnp.arange(tok_dev, dtype=jnp.int32)
    valid_rows = (positions < jnp.take(lengths, own_seq)).astype(jnp.float32)[:, None]

    def select_one(stacked):
        return jnp.einsum("k,k...->...", chosen, stacked.astype(jnp.float32)).astype(jnp.bfloat16)

    in_down = select_one(inlet_down)
    in_up = select_one(inlet_up)
    out_down = select_one(outlet_down)
    out_up = select_one(outlet_up)
    residual = tok_rows.astype(jnp.float32)
    gain_in = norm_gain.astype(jnp.float32)
    inv_in = lax.rsqrt(jnp.mean(residual * residual, axis=1, keepdims=True) + EPSILON)
    normed = (residual * inv_in * gain_in).astype(jnp.bfloat16)
    hidden_in = jnp.dot(normed, in_down, preferred_element_type=jnp.float32).astype(jnp.bfloat16)
    all_normed, all_hidden = (
        lax.all_gather(normed, "tensor", axis=0, tiled=True),
        lax.all_gather(hidden_in, "tensor", axis=0, tiled=True),
    )
    zx_matrix = full_zx.reshape(model_dim, 2 * inner_local)
    up_matrix = in_up.reshape(in_up.shape[0], 2 * inner_local)
    p_zx = jnp.dot(all_normed, zx_matrix, preferred_element_type=jnp.float32) + jnp.dot(
        all_hidden, up_matrix, preferred_element_type=jnp.float32
    )
    p_zx = p_zx.reshape(-1, 2, inner_local)
    p_bc = jnp.dot(all_normed, full_bc, preferred_element_type=jnp.float32)
    p_dt = jnp.dot(all_normed, full_dt, preferred_element_type=jnp.float32)
    mixer_weights = (x_kernel, x_offset, bc_kernel, bc_offset, dt_bias, a_log, d_skip)
    gated_act, mixer_pull = jax.vjp(partial(mixer_part, mixer_weights), p_zx, p_bc, p_dt)
    gain_rows = out_gain.astype(jnp.float32)
    squares = lax.psum(jnp.sum(gated_act * gated_act, axis=1), "tensor")
    inv_out = lax.rsqrt(squares / INNER + EPSILON)[:, None]
    normed_out = (gated_act * inv_out * gain_rows).astype(jnp.bfloat16)
    row_start = lax.axis_index("tensor") * inner_local
    down_rows = lax.dynamic_slice_in_dim(out_down, row_start, inner_local, 0)
    summed_out, summed_hidden = (
        lax.psum_scatter(
            jnp.dot(normed_out, full_out, preferred_element_type=jnp.float32),
            "tensor",
            scatter_dimension=0,
            tiled=True,
        ),
        lax.psum_scatter(
            jnp.dot(normed_out, down_rows, preferred_element_type=jnp.float32),
            "tensor",
            scatter_dimension=0,
            tiled=True,
        ),
    )
    hidden_out = summed_hidden.astype(jnp.bfloat16)
    branch_out = summed_out + jnp.dot(hidden_out, out_up, preferred_element_type=jnp.float32)
    output = (
        (residual + valid_rows * branch_out).astype(jnp.bfloat16).reshape(1, tok_dev, model_dim)
    )
    cot_rows = cotangent.reshape(tok_dev, model_dim).astype(jnp.float32)
    grad_branch = (cot_rows * valid_rows).astype(jnp.bfloat16)
    back_hidden = jnp.dot(grad_branch, out_up.T, preferred_element_type=jnp.float32).astype(
        jnp.bfloat16
    )
    outup_sum = jnp.dot(hidden_out.T, grad_branch, preferred_element_type=jnp.float32)
    wide_branch, wide_hidden = (
        lax.all_gather(grad_branch, "tensor", axis=0, tiled=True),
        lax.all_gather(back_hidden, "tensor", axis=0, tiled=True),
    )
    back_normed = jnp.dot(wide_branch, full_out.T, preferred_element_type=jnp.float32) + jnp.dot(
        wide_hidden, down_rows.T, preferred_element_type=jnp.float32
    )
    weighted_out = gain_rows * back_normed
    cross_sum = lax.psum(jnp.sum(weighted_out * gated_act, axis=1), "tensor")
    back_gated = inv_out * weighted_out - gated_act * inv_out**3 * (cross_sum / INNER)[:, None]
    local_rows = jnp.dot(normed_out.T, wide_hidden, preferred_element_type=jnp.float32)
    outdown_sum = lax.dynamic_update_slice_in_dim(
        jnp.zeros((INNER, local_rows.shape[1]), jnp.float32), local_rows, row_start, 0
    )
    grad_zx, grad_bc, grad_dt = mixer_pull(back_gated)
    low_zx3 = grad_zx.astype(jnp.bfloat16)
    low_zx = low_zx3.reshape(-1, 2 * inner_local)
    low_dt = grad_dt.astype(jnp.bfloat16)
    inup_sum = jnp.dot(all_hidden.T, low_zx, preferred_element_type=jnp.float32).reshape(
        -1, 2, inner_local
    )
    normed_part = jnp.dot(low_zx, zx_matrix.T, preferred_element_type=jnp.float32) + jnp.dot(
        low_dt, full_dt.T, preferred_element_type=jnp.float32
    )
    hidden_part = jnp.dot(low_zx, up_matrix.T, preferred_element_type=jnp.float32)
    grad_normed, grad_hidden, grad_bcrows = (
        lax.psum_scatter(normed_part, "tensor", scatter_dimension=0, tiled=True),
        lax.psum_scatter(hidden_part, "tensor", scatter_dimension=0, tiled=True),
        lax.psum_scatter(grad_bc, "tensor", scatter_dimension=0, tiled=True),
    )
    low_bc = grad_bcrows.astype(jnp.bfloat16)
    low_hidden = grad_hidden.astype(jnp.bfloat16)
    grad_normed = (
        grad_normed
        + jnp.dot(low_bc, full_bc.T, preferred_element_type=jnp.float32)
        + jnp.dot(low_hidden, in_down.T, preferred_element_type=jnp.float32)
    )
    indown_sum = jnp.dot(normed.T, low_hidden, preferred_element_type=jnp.float32)
    weighted = gain_in * grad_normed
    grad_input = (
        cot_rows
        + inv_in * weighted
        - residual * inv_in**3 * jnp.mean(weighted * residual, axis=1, keepdims=True)
    )
    sent_back = grad_input.astype(jnp.bfloat16).reshape(1, 1, tok_dev, model_dim)
    returned = lax.all_to_all(sent_back, "dp", split_axis=2, concat_axis=0, tiled=True)
    token_grads = jnp.take(returned, dealt_to, axis=0)
    inlet_dgrad, outlet_dgrad, outlet_ugrad = lax.psum(
        (
            chosen[:, None, None] * indown_sum[None],
            chosen[:, None, None] * outdown_sum[None],
            chosen[:, None, None] * outup_sum[None],
        ),
        ("dp", "tensor"),
    )
    inlet_ugrad = lax.psum(
        (chosen[:, None, None, None] * inup_sum[None]).astype(jnp.bfloat16), "dp"
    ).astype(jnp.float32)
    return (output, token_grads, inlet_dgrad, inlet_ugrad, outlet_dgrad, outlet_ugrad)


def solution(mesh):
    in_specs = (
        P(None, "tensor", "dp", None),
        P("dp", "tensor", None),
        P(),
        P(),
        P(),
        P(),
        P("dp", None, "tensor"),
        P("dp", "tensor"),
        P("dp", None),
        P(None, "tensor"),
        P("tensor"),
        P(),
        P(),
        P("tensor"),
        P("tensor"),
        P("tensor"),
        P("tensor"),
        P("tensor", "dp"),
        P(),
        P(None, None, None, "tensor"),
        P(),
        P(),
    )
    out_specs = (
        P("dp", "tensor", None),
        P(None, "tensor", "dp", None),
        P(),
        P(None, None, None, "tensor"),
        P(),
        P(),
    )
    return jax.shard_map(shards, mesh=mesh, in_specs=in_specs, out_specs=out_specs, check_vma=False)
```

profile of v0, /device:TPU:0, one launch (start us, length us, event | category | flops | bytes accessed | tf_op | source)
XLA Modules:
  0.0 787.3 jit_solution(1121650660833322522)
XLA Ops:
  17.4 7.4 all-to-all-start
  24.9 26.5 %all-to-all-done = bf16[8,1,64,768]{3,2,1,0:T(8,128)(2,1)S(1)} async-done(((bf16[8,1,64,768]{3,2,1,0:T(8,128)(2,1)}), bf16[8,1,64,768]{3,2,1,0:T(8,128)(2,1)S(1)}, u32[]{:S(2)}, u32[]{:S(2)}) %all-to-all-start) | async-done | bytes 786464 | tf_op jit(solution)/shard_map/all_to_all | solution.py:125
  56.1 26.0 %all-gather = bf16[8,96,6]{1,2,0:T(8,128)(2,1)S(1)} all-gather(bf16[1,96,6]{1,2,0:T(8,128)(2,1)S(1)} %bitcast.353), channel_id=1, replica_groups=mesh['dp'=8,'tensor'=4] {'dp'}, dimensions={0}, use_global_device_ids=true | all-gather | bytes 10368 | tf_op jit(solution)/shard_map/all_gather | solution.py:116
  85.3 5.8 all_gather.31
  93.0 31.3 %all_gather.27 = bf16[768,256]{1,0:T(8,128)(2,1)S(1)} all-gather(bf16[96,256]{1,0:T(8,128)(2,1)} %param.32), channel_id=1, replica_groups=mesh['dp'=8,'tensor'=4] {'dp'}, dimensions={0}, use_global_device_ids=true | all-gather | bytes 442368 | tf_op jit(solution)/shard_map/all_gather | solution.py:117
  126.0 31.6 %all_gather.29 = bf16[384,768]{0,1:T(8,128)(2,1)S(1)} all-gather(bf16[384,96]{0,1:T(8,128)(2,1)} %param.41), channel_id=1, replica_groups=mesh['dp'=8,'tensor'=4] {'dp'}, dimensions={1}, use_global_device_ids=true | all-gather | bytes 663552 | tf_op jit(solution)/shard_map/all_gather | solution.py:118
  158.0 5.9 all_gather.26
  166.2 5.4 fusion.223
  229.9 15.3 %bitcast_add_fusion.2 = f32[8,256,6,64]{1,3,2,0:T(8,128)S(1)} fusion(f32[8,256,6,64]{1,3,2,0:T(8,128)S(1)} %fusion.84, f32[8,256,6]{1,2,0:T(8,128)S(1)} %bitcast.332, f32[8,256,6]{1,2,0:T(8,128)S(1)} %copy-done.64, f32[8,256,256]{2,1,0:T(8,128)S(1)} %fusion.221, pred[256,256]{1,0:T(8,128)(4,1)S(1)} %copy-done.65, f32[8,256,6,64]{1,0,3,2:T(8,128)S(1)} %bitcast.297, ...), kind=kOutput, calls=%fused_computation.50 | convolution fusion | flops 2433220608 | bytes 11747328 | tf_op jit(solution)/shard_map/jvp(ctsh,cshp->cthp)/dot_general | solution.py:47
  253.6 10.0 %multiply_reduce_fusion.3 = (f32[2048]{0:T(1024)}, f32[2048]{0:T(1024)}, f32[2048,384]{1,0:T(8,128)}, f32[2048,384]{1,0:T(8,128)}) fusion(f32[2048,1,384]{2,0,1:T(8,128)} %copy.269, f32[2048,384]{1,0:T(8,128)} %copy.213, f32[2048,384]{1,0:T(8,128)} %get-tuple-element.75, f32[384]{0:T(512)} %mul.552, f32[2048,384]{1,0:T(8,128)} %fusion.223, ...), kind=kOutput, calls=%fused_computation.55 | convolution fusion | flops 38531072 | bytes 19058692 | tf_op jit(solution)/shard_map/dot_general | solution.py:197
  263.6 13.0 %all-reduce.16 = (f32[2048]{0:T(1024)}, f32[2048]{0:T(1024)}) all-reduce(f32[2048]{0:T(1024)} %get-tuple-element.57, f32[2048]{0:T(1024)} %get-tuple-element.56), channel_id=1, replica_groups=mesh['dp'=8,'tensor'=4] {'tensor'}, use_global_device_ids=true, to_apply=%region_3.5 | all-reduce | flops 4096 | bytes 32768 | tf_op jit(solution)/shard_map/psum | solution.py:163
  277.3 9.0 %fusion.24 = (f32[2048,1,384]{2,0,1:T(8,128)}, f32[2048,384]{1,0:T(8,128)}, bf16[2048,384]{1,0:T(8,128)(2,1)}) fusion(f32[2048,1,384]{2,0,1:T(8,128)} %copy.269, f32[2048]{0:T(1024)S(1)} %get-tuple-element.106, f32[2048,384]{1,0:T(8,128)} %get-tuple-element.73, f32[2048]{0:T(1024)S(1)} %get-tuple-element.93, f32[2048,384]{1,0:T(8,128)} %get-tuple-element.103, ...), kind=kLoop, calls=%fused_computation.34 | loop fusion | flops 19660800 | bytes 23620608 | tf_op jit(solution)/shard_map/transpose(jvp())/broadcast_in_dim | solution.py:85
  293.8 7.0 fusion.88
  304.6 5.9 fusion.211
  313.0 7.0 fusion.91
  320.0 4.5 fusion.78
  325.3 24.8 %fusion.9 = (f32[8,256,6]{1,2,0:T(8,128)}, f32[8,256,6]{1,2,0:T(8,128)}, f32[8,256,6]{1,2,0:T(8,128)}, f32[8,256,256]{2,1,0:T(8,128)S(1)}) fusion(f32[8,256,6]{1,2,0:T(8,128)} %bitcast.330, f32[8,256,6]{1,2,0:T(8,128)} %copy.199, f32[8,256,256]{2,1,0:T(8,128)} %copy-done.32, pred[256,256]{1,0:T(8,128)(4,1)} %iota_compare_fusion, ...), kind=kOutput, calls=%fused_computation.14 | convolution fusion | flops 2462543872 | bytes 10797056 | tf_op jit(solution)/shard_map/transpose(jvp(ctsh,cshp->cthp))/dot_general | solution.py:47
  359.2 14.2 %bitcast_add_fusion.1 = f32[8,256,6,64]{1,3,2,0:T(8,128)S(1)} fusion(f32[8,256,6,64]{1,3,2,0:T(8,128)} %fusion.78, f32[8,256,6]{1,2,0:T(8,128)} %bitcast.331, f32[8,256,6]{1,2,0:T(8,128)} %copy.199, f32[8,256,256]{2,1,0:T(8,128)} %copy-done.32, pred[256,256]{1,0:T(8,128)(4,1)} %iota_compare_fusion, f32[8,6,64,256]{3,0,2,1:T(8,128)} %bitcast.304, ...), kind=kOutput, calls=%fused_computation.43 | convolution fusion | flops 2433220608 | bytes 11747328 | tf_op jit(solution)/shard_map/transpose(jvp(ctsh,cshp->cthp))/dot_general | solution.py:47
  428.5 50.1 %reduce-scatter.10.cloned.1.call-done = f32[512,768]{1,0:T(8,128)} async-done(((f32[2048,768]{1,0:T(8,128)}), f32[512,768]{1,0:T(8,128)}) %reduce-scatter.10.cloned.1.call-update) | async-done | bytes 1572880 | tf_op jit(solution)/shard_map/reduce_scatter | solution.py:219
  484.2 6.5 reduce.13
  491.8 5.7 all-to-all-start.1
  504.4 70.8 %all-reduce.20.cloned.1.call-done = bf16[8,16,2,384]{3,2,1,0:T(2,128)(2,1)} async-done(((bf16[8,16,2,384]{3,2,1,0:T(2,128)(2,1)}), bf16[8,16,2,384]{3,2,1,0:T(2,128)(2,1)}) %all-reduce.20.cloned.1.call-update) | async-done | bytes 196624 | tf_op jit(solution)/shard_map/psum | solution.py:248
  577.0 58.3 %reduce-scatter.6.cloned.1.call-done = f32[512,768]{1,0:T(8,128)} async-done(((f32[2048,768]{1,0:T(8,128)}), f32[512,768]{1,0:T(8,128)}) %reduce-scatter.6.cloned.1.call-update) | async-done | bytes 1572880 | tf_op jit(solution)/shard_map/reduce_scatter | solution.py:169
  640.6 133.8 %all-reduce.22.cloned.1.call-done = (f32[8,768,16]{1,2,0:T(8,128)}, f32[8,1536,16]{1,2,0:T(8,128)}, f32[8,16,768]{2,1,0:T(8,128)}) async-done(((f32[8,768,16]{1,2,0:T(8,128)}, f32[8,1536,16]{1,2,0:T(8,128)}, f32[8,16,768]{2,1,0:T(8,128)}), (f32[8,768,16]{1,2,0:T(8,128)}, f32[8,1536,16]{1,2,0:T(8,128)}, f32[8,16,768]{2,1,0:T(8,128)})) %all-reduce.22.cloned.1.call-update) | async-done | bytes 1572880 | tf_op jit(solution)/shard_map/psum | solution.py:240
  (364 shorter events, 193.6 us)
Async XLA Ops:
  7.2 156.6 %all-gather.7.cloned.1.call-start = ((), (), s32[]{:S(2)}) async-start(), calls=%async_computation.8 | async-start | bytes 1327104 | tf_op jit(solution)/shard_map/all_gather | solution.py:115
  8.9 157.3 %all-gather.9.cloned.1.call-start = ((), (), s32[]{:S(2)}) async-start(), calls=%async_computation.11 | async-start | bytes 3932160 | tf_op jit(solution)/shard_map/all_gather | solution.py:194
  16.4 66.7 %copy-start.56 = (bf16[8,768,16]{1,2,0:T(8,128)(2,1)S(1)}, bf16[8,768,16]{1,2,0:T(8,128)(2,1)}, u32[]{:S(2)}) copy-start(bf16[8,768,16]{1,2,0:T(8,128)(2,1)} %param.42) | copy-start | bytes 589828
  17.4 66.1 %copy-start.48 = (bf16[8,1536,16]{1,2,0:T(8,128)(2,1)S(1)}, bf16[8,1536,16]{1,2,0:T(8,128)(2,1)}, u32[]{:S(2)}) copy-start(bf16[8,1536,16]{1,2,0:T(8,128)(2,1)} %param.44) | copy-start | bytes 1179652
  17.4 67.4 %copy-start.57 = (bf16[8,16,768]{2,1,0:T(8,128)(2,1)S(1)}, bf16[8,16,768]{2,1,0:T(8,128)(2,1)}, u32[]{:S(2)}) copy-start(bf16[8,16,768]{2,1,0:T(8,128)(2,1)} %param.45) | copy-start | bytes 589828
  17.4 67.6 %copy-start.19 = (bf16[512,768]{1,0:T(8,128)(2,1)S(1)}, bf16[512,768]{1,0:T(8,128)(2,1)}, u32[]{:S(2)}) copy-start(bf16[512,768]{1,0:T(8,128)(2,1)} %fusion.62) | copy-start | bytes 2359300
  17.4 34.0 %all-to-all-start = ((bf16[8,1,64,768]{3,2,1,0:T(8,128)(2,1)}), bf16[8,1,64,768]{3,2,1,0:T(8,128)(2,1)S(1)}, u32[]{:S(2)}, u32[]{:S(2)}) async-start(bf16[8,1,64,768]{3,2,1,0:T(8,128)(2,1)} %bitcast_select_fusion.1), calls=%async_computation | async-start | bytes 1572864 | tf_op jit(solution)/shard_map/all_to_all | solution.py:125
  24.8 66.9 %copy-start.90 = (f32[4,384]{1,0:T(4,128)S(1)}, f32[4,384]{1,0:T(4,128)}, u32[]{:S(2)}) copy-start(f32[4,384]{1,0:T(4,128)} %param.33) | copy-start | bytes 18436
  24.8 146.8 %all-gather.5.cloned.1.call-start = ((), (), s32[]{:S(2)}) async-start(), calls=%async_computation.7 | async-start | bytes 3932160 | tf_op jit(solution)/shard_map/all_gather | solution.py:149
  51.7 73.8 %copy-start.91 = (f32[4,256]{1,0:T(4,128)S(1)}, f32[4,256]{1,0:T(4,128)}, u32[]{:S(2)}) copy-start(f32[4,256]{1,0:T(4,128)} %param.35) | copy-start | bytes 12292
  53.5 104.2 %copy-start.21 = (bf16[512,768]{1,0:T(8,128)(2,1)S(1)}, bf16[512,768]{1,0:T(8,128)(2,1)}, u32[]{:S(2)}) copy-start(bf16[512,768]{1,0:T(8,128)(2,1)} %fusion.67) | copy-start | bytes 2359300
  53.5 373.6 %reduce-scatter.12.cloned.1.call-start = ((), (), s32[]{:S(2)}) async-start(), calls=%async_computation.13 | async-start | bytes 2621440 | tf_op jit(solution)/shard_map/reduce_scatter | solution.py:221
  83.5 82.7 %copy-start.37 = (bf16[1,768,16]{2,1,0:T(8,128)(2,1)}, bf16[1,768,16]{2,1,0:T(8,128)(2,1)S(1)}, u32[]{:S(2)}) copy-start(bf16[1,768,16]{2,1,0:T(8,128)(2,1)S(1)} %copy.244) | copy-start | bytes 73732
  359.1 69.4 %reduce-scatter.14.cloned.1.call-start = ((), (), s32[]{:S(2)}) async-start(), calls=%async_computation.14 | async-start | bytes 163840 | tf_op jit(solution)/shard_map/reduce_scatter | solution.py:220
  402.1 76.5 %reduce-scatter.10.cloned.1.call-start = ((), (), s32[]{:S(2)}) async-start(), calls=%async_computation.12 | async-start | bytes 7864320 | tf_op jit(solution)/shard_map/reduce_scatter | solution.py:219
  410.0 91.3 %reduce-scatter.8.cloned.1.call-start = ((), (), s32[]{:S(2)}) async-start(), calls=%async_computation.10 | async-start | bytes 163840 | tf_op jit(solution)/shard_map/reduce_scatter | solution.py:175
  415.8 159.3 %all-reduce.20.cloned.1.call-start = ((), (), s32[]{:S(2)}) async-start(), calls=%async_computation.15 | async-start | bytes 393216 | tf_op jit(solution)/shard_map/psum | solution.py:248
  419.9 215.4 %reduce-scatter.6.cloned.1.call-start = ((), (), s32[]{:S(2)}) async-start(), calls=%async_computation.9 | async-start | bytes 7864320 | tf_op jit(solution)/shard_map/reduce_scatter | solution.py:169
  491.7 143.6 %copy-start.54 = (bf16[1,16,768]{2,0,1:T(2,128)(2,1)S(1)}, bf16[1,16,768]{2,0,1:T(2,128)(2,1)}, u32[]{:S(2)}) copy-start(bf16[1,16,768]{2,0,1:T(2,128)(2,1)} %copy-done.53) | copy-start | bytes 73732
  491.8 143.6 %copy-start.78 = (f32[512]{0:T(512)S(1)}, f32[512]{0:T(512)}, u32[]{:S(2)}) copy-start(f32[512]{0:T(512)} %copy-done.77) | copy-start | bytes 6148
  491.8 146.3 %all-to-all-start.1 = ((bf16[8,2,24576]{2,1,0:T(2,128)(2,1)}), bf16[8,2,24576]{2,1,0:T(2,128)(2,1)S(1)}, u32[]{:S(2)}, u32[]{:S(2)}) async-start(bf16[8,2,24576]{2,1,0:T(2,128)(2,1)} %reshape.388), calls=%async_computation.6 | async-start | bytes 1572864 | tf_op jit(solution)/shard_map/all_to_all | solution.py:238
  497.4 277.0 %all-reduce.22.cloned.1.call-start = ((), (), s32[]{:S(2)}) async-start(), calls=%async_computation.16 | async-start | bytes 3145728 | tf_op jit(solution)/shard_map/psum | solution.py:240
  501.3 134.0 %copy-start.59 = (f32[512,16]{0,1:T(8,128)S(1)}, f32[512,16]{0,1:T(8,128)}, u32[]{:S(2)}) copy-start(f32[512,16]{0,1:T(8,128)} %reduce-scatter.8.cloned.1.call-done) | copy-start | bytes 98308
  639.0 141.0 %copy-start.1 = (bf16[8,1,64,768]{3,2,1,0:T(8,128)(2,1)S(1)}, bf16[8,1,64,768]{3,2,1,0:T(8,128)(2,1)}, u32[]{:S(2)}) copy-start(bf16[8,1,64,768]{3,2,1,0:T(8,128)(2,1)} %param.24) | copy-start | bytes 2359300
  (91 other events, 938.8 us)
Sparse Core Ops, SparseCore 0:
  10.8 49.3 all-gather.6
  62.3 27.2 all-gather.8
  91.8 28.8 all-gather.4
  359.2 27.7 reduce-scatter.11
  402.2 15.5 reduce-scatter.13
  420.2 58.3 reduce-scatter.9
  481.7 19.5 reduce-scatter.7
  504.6 70.4 all-reduce.19
  577.9 57.4 reduce-scatter.5
  641.4 132.9 all-reduce.21
where the time goes:
time: 792 us; the launch traced here: 787 us
  waiting for transfers between devices  344 us (43%)
  matrix products  158 us (20%)
  blocking collectives  113 us (14%)
  local copies, waits for them, and re-layouts  83.5 us (11%)
  other arithmetic  56.7 us (7%)
  between operations  18 us (2%)
  starting transfers between devices  13.7 us (2%)
    psum x1, waiting for transfers between devices, shards(): lax.psum((chosen[:, None, None] * indown_sum[None], chosen[:, None, None]...  134 us
    psum x1, waiting for transfers between devices, shards(): lax.psum((chosen[:, None, None, None] * inup_sum[None]).astype(jnp.bfloat...  70.8 us
    reduce_scatter x1, waiting for transfers between devices, shards(): lax.psum_scatter(jnp.dot(normed_out, full_out, preferred_element_type=jnp...  58.3 us
    dot_general x3, matrix products, state_mixer(): inside = jnp.einsum('ctsh,cshp->cthp', weights, block_x, precision=HIGHEST)  54.3 us
    reduce_scatter x1, waiting for transfers between devices, shards(): lax.psum_scatter(normed_part, 'tensor', scatter_dimension=0, tiled=True)  50.1 us
    unnamed x223, local copies, waits for them, and re-layouts  36.8 us
    all_gather x1, blocking collectives, shards(): lax.all_gather(w_out, 'dp', axis=1, tiled=True)  31.6 us
    all_gather x1, blocking collectives, shards(): lax.all_gather(w_bc, 'dp', axis=0, tiled=True)  31.3 us
  transfers between devices with their start and end apart: 12, of which 6 were waited for; matrix products, arithmetic and copies ran while one was open for 14% of the time, Pallas kernels for 0%

commit v1 on v0

v1 whole, which is shorter than its diff:
```python
from functools import partial
from types import SimpleNamespace

import jax
import jax.numpy as jnp
from jax import lax
from jax.experimental import pallas as pl
from jax.experimental.pallas import tpu as pltpu
from jax.sharding import PartitionSpec as P

EPSILON = 1e-05
LOG2E = 1.4426950408889634
HIGHEST = lax.Precision.HIGHEST
MESH = pl.DeviceIdType.MESH
f32, bf16 = jnp.float32, jnp.bfloat16

BLOCKS = 4
WIDE = 384
HEADS_B = 6
SLOT = 16
CHUNK = 128
HALO = 16
ADAPTERS = 8
TOK_AT = 2
LOADED = (
    "w_zx",
    "w_dt_in",
    "x_kernel",
    "x_offset",
    "out_gain",
    "dt_bias",
    "a_log",
    "d_skip",
    "inlet_up",
    "tokens",
    "cot",
    "gain",
    "bc_kernel",
    "bc_offset",
    "inlet_down",
    "outlet_up",
    "outlet_down",
)


def nn(a, b):
    return jnp.dot(a, b, preferred_element_type=f32)


def nt(a, b):
    return lax.dot_general(a, b, (((1,), (1,)), ((), ())), preferred_element_type=f32)


def tn(a, b):
    return lax.dot_general(a, b, (((0,), (0,)), ((), ())), preferred_element_type=f32)


def two_part(v):
    high = v.astype(bf16)
    return jnp.concatenate([high, (v - high.astype(f32)).astype(bf16)], axis=1)


def sigmoid(v):
    return 1.0 / (1.0 + jnp.exp(-v))


def thirds(v):
    return v[:, :128] + v[:, 128:256] + v[:, 256:384]


def loop(count, body):
    lax.fori_loop(0, count, lambda i, carry: (body(i), carry)[1], 0)


def remote(src, dst, ssem, rsem, peer):
    return pltpu.make_async_remote_copy(src, dst, ssem, rsem, device_id=peer, device_id_type=MESH)


class Spread:
    def __init__(self, buf, ssem, rsem, piece, dp, tp, dp_size, all_blocks):
        self.buf, self.ssem, self.rsem, self.piece = buf, ssem, rsem, piece
        self.dp, self.tp, self.nz, self.n = dp, tp, dp_size // 2, dp_size
        self.z, self.y = lax.div(dp, 2), lax.rem(dp, 2)
        self.all_blocks = all_blocks
        self.core = tp + 1 - 2 * lax.rem(tp, 2)
        self.far = lax.rem(tp + 2, 4)
        self.far_core = lax.rem(self.core + 2, 4)

    def at(self, t, d):
        rows = pl.ds(pl.multiple_of(d * self.piece, 16), self.piece)
        return self.buf.at[t, rows, :] if self.all_blocks else self.buf.at[rows, :]

    def copy(self, kind, t, d):
        peer = (
            (jnp.minimum(self.dp + 2, self.n - 1), self.tp),
            (jnp.maximum(self.dp - 2, 0), self.tp),
            (self.dp + 1 - 2 * self.y, self.tp),
            (self.dp, self.far),
            (self.dp, self.core),
            (self.dp, self.core),
        )[kind]
        rsem = self.rsem.at[t, d] if self.all_blocks else self.rsem.at[d]
        return remote(self.at(t, d), self.at(t, d), self.ssem.at[kind, d], rsem, peer)

    def wait(self, t, d):
        self.copy(2, t, d).wait_recv()

    def sideways(self, d):
        self.copy(2, self.tp, d).start()
        self.across(d)

    def across(self, d):
        if self.all_blocks:
            self.copy(3, self.tp, d).start()

    def column(self, t):
        peer = (self.dp, self.core)
        return remote(self.buf.at[t], self.buf.at[t], self.ssem.at[4, 0], self.rsem.at[t, 0], peer)

    def begin(self):
        @pl.when(self.z < self.nz - 1)
        def _():
            self.copy(0, self.tp, self.dp).start()

        @pl.when(self.z > 0)
        def _():
            self.copy(1, self.tp, self.dp).start()

        self.sideways(self.dp)

    def hop(self, k):
        low, high = self.dp - 2 * k, self.dp + 2 * k

        @pl.when(self.z >= k)
        def _():
            self.wait(self.tp, low)

            @pl.when(self.z < self.nz - 1)
            def _():
                self.copy(0, self.tp, low).start()

            self.sideways(low)

        @pl.when(self.z + k < self.nz)
        def _():
            self.wait(self.tp, high)

            @pl.when(self.z > 0)
            def _():
                self.copy(1, self.tp, high).start()

            self.sideways(high)

    def from_y(self, k):
        other = 1 - 2 * self.y
        low, high = self.dp + other - 2 * k, self.dp + other + 2 * k

        @pl.when(self.z >= k)
        def _():
            self.wait(self.tp, low)
            self.across(low)

        if k:

            @pl.when(self.z + k < self.nz)
            def _():
                self.wait(self.tp, high)
                self.across(high)

    def own_done(self):
        self.column(self.tp).start()

    def from_x(self):
        def forward(d):
            self.wait(self.far, d)
            self.copy(5, self.far, d).start()

        other = 1 - 2 * self.y
        for k in range(self.nz + 1):
            for shift, reach in ((0, k), (other, k - 1)):
                low, high = self.dp + shift - 2 * reach, self.dp + shift + 2 * reach
                if 0 <= reach < self.nz:

                    @pl.when(self.z >= reach)
                    def _(low=low):
                        forward(low)

                    if reach:

                        @pl.when(self.z + reach < self.nz)
                        def _(high=high):
                            forward(high)

    def from_core(self):
        self.column(self.core).wait_recv()
        self.from_far_core()

    def from_far_core(self):
        for k in range(self.n):
            self.wait(self.far_core, lax.rem(self.dp + k, self.n))

    def finish(self):
        for zz in range(self.nz):
            d = 2 * zz + self.y

            @pl.when(jnp.logical_and(self.z >= zz, self.z < self.nz - 1))
            def _():
                self.copy(0, self.tp, d).wait_send()

            @pl.when(jnp.logical_and(self.z <= zz, self.z > 0))
            def _():
                self.copy(1, self.tp, d).wait_send()

            self.copy(2, self.tp, d).wait_send()
        if self.all_blocks:
            for d in range(self.n):
                self.copy(3, self.tp, d).wait_send()
                self.copy(5, self.far, d).wait_send()
            self.column(self.tp).wait_send()


class Toward:
    def __init__(self, me, size, peer, src, dst, ssem, rsem):
        self.me, self.size, self.peer = me, size, peer
        self.src, self.dst, self.ssem, self.rsem = src, dst, ssem, rsem

    def copy(self, to, sender):
        return remote(self.src(to), self.dst(sender), self.ssem.at[to], self.rsem.at[sender], self.peer(to))

    def others(self):
        return [lax.rem(self.me + k, self.size) for k in range(1, self.size)]

    def start(self):
        for to in self.others():
            self.copy(to, self.me).start()

    def wait(self):
        for sender in self.others():
            self.copy(sender, sender).wait_recv()

    def finish(self):
        for to in self.others():
            self.copy(to, self.me).wait_send()


def front(r, dp, tp, dp_size, tp_size, load, scalars, work):
    block = r.tok_out.shape[1]
    rows_n = r.gbr.shape[0]
    piece = r.w_dt_in.shape[1]
    own_rows = pl.ds(pl.multiple_of(piece * dp, 16), piece)

    def place(d):
        return pl.ds(pl.multiple_of(HALO + block * d, 16), block)

    r.dts[tp, dp] = jnp.zeros_like(r.dts[tp, dp])
    r.small[tp] = jnp.zeros_like(r.small[tp])
    r.wdt[...] = jnp.zeros_like(r.wdt)
    own_out = pltpu.make_async_copy(r.w_out, r.wout.at[tp, own_rows, :], r.own_sem.at[0])
    own_bc = pltpu.make_async_copy(r.w_bc, r.wbc.at[own_rows, :], r.own_sem.at[1])
    own_out.start()
    own_bc.start()
    load.wait("w_zx")
    for k in range(2):
        r.zx[tp, own_rows, k * WIDE : (k + 1) * WIDE] = r.w_zx[:, k, :]
    own_bc.wait()
    work.greet()

    def to_dp(d):
        return (d, tp)

    def to_tp(t):
        return (dp, t)

    zx = Spread(r.zx, r.zx_ss, r.zx_rs, piece, dp, tp, dp_size, True)
    wout = Spread(r.wout, r.wo_ss, r.wo_rs, piece, dp, tp, dp_size, True)
    wbc = Spread(r.wbc, r.bc_ss, r.bc_rs, piece, dp, tp, dp_size, False)
    tok = Toward(dp, dp_size, to_dp, lambda d: r.tok_out.at[d], lambda d: r.ext.at[place(d), :], r.tok_ss, r.tok_rs)
    dts = Toward(dp, dp_size, to_dp, lambda d: r.dts.at[tp, dp], lambda d: r.dts.at[tp, d], r.dt_ss, r.dt_rs)
    dts2 = Toward(tp, tp_size, to_tp, lambda t: r.dts.at[tp], lambda t: r.dts.at[t], r.d2_ss, r.d2_rs)
    ups = Toward(tp, tp_size, to_tp, lambda t: r.up.at[tp], lambda t: r.up.at[t], r.up_ss, r.up_rs)
    smalls = Toward(tp, tp_size, to_tp, lambda t: r.small.at[tp], lambda t: r.small.at[t], r.sm_ss, r.sm_rs)

    zx.begin()
    wbc.begin()
    load.wait("w_dt_in", "x_kernel", "x_offset", "out_gain", "dt_bias", "a_log", "d_skip", "inlet_up")
    r.dts[tp, dp, 0:HEADS_B, 0:piece] = r.w_dt_in[...]
    r.small[tp, 0:4, :] = r.x_kernel[...]
    r.small[tp, 4, :] = r.x_offset[...]
    r.small[tp, 5, :] = r.out_gain[...].astype(f32)
    r.small[tp, 6, 0:HEADS_B] = r.dt_bias[...]
    r.small[tp, 7, 0:HEADS_B] = r.a_log[...]
    r.small[tp, 8, 0:HEADS_B] = r.d_skip[...]
    adapter = scalars.adapter()
    for k in range(2):
        r.up[tp, :, k * WIDE : (k + 1) * WIDE] = r.inlet_up[adapter, :, k, :]
    dts.start()
    ups.start()
    smalls.start()
    load.wait("tokens")
    for g in range(dp_size):
        r.tok_out[g] = r.tokens[scalars.seq_of(g)]
    r.ext[place(dp), :] = r.tok_out[dp]
    for k in range(1, zx.nz):
        zx.hop(k)
        zx.from_y(k - 1)
        if k == TOK_AT:
            tok.start()
        wbc.hop(k)
        wbc.from_y(k - 1)
    dts.wait()
    dts2.start()
    zx.from_y(zx.nz - 1)
    zx.own_done()
    wbc.from_y(zx.nz - 1)
    own_out.wait()
    wout.begin()
    work.early()
    dts2.wait()
    ups.wait()
    smalls.wait()
    for d in range(dp_size):
        lines = jnp.concatenate([r.dts[t, d].astype(f32) for t in range(BLOCKS)] * 2, axis=0)
        r.wdt[d * piece : (d + 1) * piece, :] = lines.T[:piece].astype(bf16)
    tok.wait()
    edge = remote(
        r.ext.at[rows_n : rows_n + HALO, :],
        r.ext.at[0:HALO, :],
        r.ha_ss.at[0],
        r.ha_rs.at[0],
        (dp, lax.rem(tp + 1, tp_size)),
    )

    @pl.when(tp < tp_size - 1)
    def _():
        edge.start()

    work.norm_own()

    @pl.when(tp > 0)
    def _():
        edge.wait_recv()

    @pl.when(tp == 0)
    def _():
        r.ext[0:HALO, :] = jnp.zeros((HALO, r.ext.shape[1]), bf16)

    work.norm_edge()
    work.project(tp)
    zx.from_x()
    wout.hop(1)
    wout.from_y(0)
    zx.column(zx.core).wait_recv()
    work.project(zx.core)
    work.project_bc()
    wout.hop(2)
    wout.from_y(1)
    work.project(zx.far)
    zx.from_far_core()
    wout.hop(3)
    wout.from_y(2)
    wout.from_y(3)
    wout.own_done()
    work.project(zx.far_core)

    def end():
        for part in (zx, wbc, wout, tok, dts, dts2, ups, smalls):
            part.finish()

        @pl.when(tp < tp_size - 1)
        def _():
            edge.wait_send()

    return wout, end


class Returns:
    def __init__(self, r, dp, tp, dp_size):
        self.r, self.dp, self.tp, self.n = r, dp, tp, dp_size
        self.block = r.tok_out.shape[1]

    def rows(self, d):
        return pl.ds(pl.multiple_of(self.block * d, 16), self.block)

    def copy(self, d, sender):
        r = self.r
        return remote(r.tg.at[self.rows(d), :], r.tg_in.at[sender], r.tg_ss.at[d], r.tg_rs.at[sender], (d, self.tp))

    def own(self):
        r = self.r
        return pltpu.make_async_copy(r.tg.at[self.rows(self.dp), :], r.tg_in.at[self.dp], r.own_sem.at[2])

    def send(self, d):
        @pl.when(d != self.dp)
        def _():
            self.copy(d, self.dp).start()

        @pl.when(d == self.dp)
        def _():
            self.own().start()

    def others(self):
        return [lax.rem(self.dp + k, self.n) for k in range(1, self.n)]

    def finish(self):
        self.own().wait()
        for d in self.others():
            self.copy(d, d).wait_recv()
        for d in self.others():
            self.copy(d, self.dp).wait_send()


class Sums:
    def __init__(self, r, dp, tp, dp_size, tp_size, part):
        self.r, self.dp, self.tp, self.part = r, dp, tp, part

        def to_tp(t):
            return (dp, t)

        def to_dp(d):
            return (d, tp)

        sems = ((r.ga_ss, r.ga_rs), (r.gb_ss, r.gb_rs))[part]
        sends = ((r.gc_ss, r.gc_rs), (r.gd_ss, r.gd_rs))[part]
        dst = (r.all_up, r.all_rest)[part]
        self.first = Toward(tp, tp_size, to_tp, lambda t: r.sum_out.at[part, t], lambda t: r.sum_in.at[part, t], *sems)
        self.second = Toward(
            dp,
            dp_size,
            to_dp,
            lambda d: r.sum_all.at[part],
            lambda d: dst.at[d] if part == 0 else dst.at[tp, d],
            *sends,
        )
        self.own = pltpu.make_async_copy(
            r.sum_all.at[part], dst.at[dp] if part == 0 else dst.at[tp, dp], r.own_sem.at[3 + part]
        )
        self.core = tp + 1 - 2 * lax.rem(tp, 2)
        self.far = lax.rem(tp + 2, 4)

    def start(self):
        self.first.start()

    def middle(self):
        r, part = self.r, self.part
        r.sum_in[part, self.tp] = r.sum_out[part, self.tp]
        self.first.wait()
        total = r.sum_in[part, 0].astype(f32)
        for t in range(1, BLOCKS):
            total = total + r.sum_in[part, t].astype(f32)
        r.sum_all[part] = total.astype(bf16)
        self.second.start()
        self.own.start()

    def hop(self, kind, t, peer):
        rest = self.r.all_rest.at[t]
        return remote(rest, rest, self.r.g3_ss.at[kind], self.r.g3_rs.at[t], (self.dp, peer))

    def gathered(self):
        self.second.wait()
        self.own.wait()
        if self.part:
            self.hop(0, self.tp, self.far).start()
            self.hop(1, self.tp, self.core).start()

    def pass_on(self):
        self.hop(0, self.far, self.far).wait_recv()
        self.hop(2, self.far, self.core).start()

    def finish(self):
        if self.part:
            self.hop(1, self.core, self.core).wait_recv()
            self.hop(2, lax.rem(self.core + 2, 4), self.core).wait_recv()
            for kind, t in ((0, self.tp), (1, self.tp), (2, self.far)):
                self.hop(kind, t, self.core).wait_send()
        self.first.finish()
        self.second.finish()


class Loads:
    def __init__(self, r, names):
        self.copies = {}
        for i, name in enumerate(names):
            src, dst = getattr(r, name), getattr(r, "v_" + name)
            self.copies[name] = pltpu.make_async_copy(src, dst, r.load_sem.at[i])
            setattr(r, name, dst)

    def start(self):
        for copy in self.copies.values():
            copy.start()

    def wait(self, *names):
        for name in names:
            self.copies[name].wait()


def mixer_kernel(direct, names, *refs):
    r = SimpleNamespace(**dict(zip(names, refs)))
    dp, tp = lax.axis_index("dp"), lax.axis_index("tensor")
    tp_size = lax.axis_size("tensor")
    lengths, dealt, adapters = r.lengths, r.dealt_to, r.adapter_id
    rows_n = r.cot.shape[0]
    chunks = rows_n // CHUNK
    after, before = lax.rem(tp + 1, tp_size), lax.rem(tp + tp_size - 1, tp_size)

    dp_size = lax.axis_size("dp")
    barrier = pltpu.get_barrier_semaphore()
    peers = [(dp, after), (dp, before)]
    if direct:
        peers = [(dp, lax.rem(tp + k, tp_size)) for k in range(1, tp_size)]
        peers += [(lax.rem(dp + k, dp_size), tp) for k in range(1, dp_size)]
    for peer in peers:
        pl.semaphore_signal(barrier, inc=1, device_id=peer, device_id_type=MESH)

    def greet():
        pl.semaphore_wait(barrier, len(peers))

    def seq_of(g):
        seq = jnp.int32(0)
        for s in range(dealt.shape[0]):
            seq = jnp.where(dealt[s] == g, s, seq)
        return seq

    own = seq_of(dp)
    adapter, length = adapters[own], lengths[own]
    if direct:
        r.tg = r.gbr
        load = Loads(r, LOADED)
        load.start()
    else:
        r.out_rows = r.out
        greet()

    ext, nrm, hid, zx, up = r.ext, r.nrm, r.hid, r.zx, r.up
    gate, spz, px, xs, spx, xd = r.gate, r.spz, r.px, r.xs, r.spx, r.xd
    expand, small, pb, pd = r.expand, r.small, r.pb, r.pd
    dth, ech, tlh, eth, cu, cut, tot = r.dth, r.ech, r.tlh, r.eth, r.cu, r.cut, r.tot
    ub, bb, cb, bt, ct, sc = r.ub, r.bb, r.cb, r.bt, r.ct, r.sc
    st, rt, y, gy, gzx, xp = r.st, r.rt, r.y, r.gy, r.gzx, r.px

    def rows(c, base=0, size=CHUNK):
        return pl.ds(pl.multiple_of(c * CHUNK + base, 16), size)

    def valid(c):
        at = tp * rows_n + c * CHUNK + lax.broadcasted_iota(jnp.int32, (CHUNK, 1), 0)
        return jnp.where(at < length, 1.0, 0.0).astype(f32)

    def fill_expand(b):
        head = jnp.bitwise_and(lax.broadcasted_iota(jnp.int32, (256, WIDE), 0), 127)
        lane = lax.broadcasted_iota(jnp.int32, (256, WIDE), 1)
        expand[b] = jnp.where(head == SLOT * b + lax.shift_right_logical(lane, 6), 1.0, 0.0).astype(bf16)

    def take_adapter():
        r.idn[...] = r.inlet_down[adapter]
        r.oup[...] = r.outlet_up[adapter]
        for b in range(BLOCKS):
            r.odn[b] = r.outlet_down[adapter, :, b * WIDE : (b + 1) * WIDE]

    cot, gbr, ghid, wout = r.cot, r.gbr, r.ghid, r.wout

    def mask_cot(c):
        gbr[rows(c), :] = (cot[rows(c), :].astype(f32) * valid(c)).astype(bf16)

    def early():
        if direct:
            load.wait("cot", "gain", "bc_kernel", "bc_offset", "inlet_down", "outlet_up", "outlet_down")
        take_adapter()
        loop(BLOCKS, fill_expand)
        loop(chunks, mask_cot)
        ghid[...] = nt(gbr[...], r.oup[...]).astype(bf16)
        r.ghid_t[...] = nt(r.oup[...], gbr[...]).astype(bf16)

    def norm_rows(at, size):
        u = ext[pl.ds(at, size), :].astype(f32)
        inv = lax.rsqrt(jnp.mean(u * u, axis=1, keepdims=True) + EPSILON)
        nrm[pl.ds(at, size), :] = (u * inv * r.gain[...].astype(f32)[None]).astype(bf16)

    def norm_own():
        loop(chunks, lambda c: norm_rows(pl.multiple_of(c * CHUNK + HALO, 16), CHUNK))

    def norm_edge():
        norm_rows(0, HALO)
        hid[...] = nt(nrm[...], r.idn[...]).astype(bf16)

    def project(b):
        p = nn(nrm[...], zx[b]) + nn(hid[...], up[b])
        gate[b] = p[HALO:, :WIDE]
        px[b] = p[:, WIDE:]

    low_tri = lax.broadcasted_iota(jnp.int32, (CHUNK, CHUNK), 0) >= lax.broadcasted_iota(
        jnp.int32, (CHUNK, CHUNK), 1
    )

    def head_lanes():
        total = small[0, :, :128]
        for b in range(1, BLOCKS):
            total = total + pltpu.roll(small[b, :, :128], SLOT * b, 1)
        return total

    def steps(c):
        tri = jnp.where(low_tri, 1.0, 0.0).astype(f32)
        p = pd[rows(c), :]
        e = jnp.exp(-jnp.abs(p))
        log1p = jnp.where(e < 0.01, e * (1.0 - e * (0.5 - e * (1.0 / 3.0))), jnp.log(1.0 + e))
        dt = jnp.maximum(p, 0.0) + log1p
        rate = r.decay[0:1, :] * LOG2E
        cum = jnp.dot(tri, dt * rate, precision=HIGHEST, preferred_element_type=f32)
        total = cum[CHUNK - 1 : CHUNK]
        cu[rows(c), :] = cum
        cut[c] = cum.T
        tot[pl.ds(c, 1), :] = total
        dth[rows(c), :] = two_part(dt)
        ech[rows(c), :] = two_part(jnp.exp2(cum))
        tlh[rows(c), :] = two_part(jnp.exp2(total - cum))

    bc_kernel, bc_offset = r.bc_kernel, r.bc_offset

    def conv(window, kernel_row, offset):
        total = offset + kernel_row(3) * window[8:]
        for j in range(3):
            shifted = pltpu.roll(window, window.shape[0] - (5 + j), 0)
            total = total + kernel_row(j) * shifted[:CHUNK]
        return total

    def make_bc(c):
        window = pb[pl.ds(pl.multiple_of(c * CHUNK + 8, 8), CHUNK + 8), :]
        u = conv(window, lambda j: bc_kernel[j : j + 1, :], bc_offset[...][None])
        v = u * sigmoid(u)
        ub[rows(c), :] = u
        b_rows, c_rows = v[:, :128], v[:, 128:]
        bb[rows(c), :] = b_rows.astype(bf16)
        cb[rows(c), :] = c_rows.astype(bf16)
        bt[c] = b_rows.T.astype(bf16)
        ct[c] = c_rows.T.astype(bf16)
        sc[c] = jnp.where(low_tri, nt(c_rows.astype(bf16), b_rows.astype(bf16)), 0.0)

    def project_bc():
        head_rows = head_lanes()
        r.decay[...] = jnp.broadcast_to(-jnp.exp(head_rows[7:8]), (8, 128))
        r.skip[...] = two_part(head_rows)
        pb[...] = nn(nrm[...], r.wbc[...])
        pd[...] = nn(nrm[HALO:, :], r.wdt[...]) + head_rows[6:7]
        tot[...] = jnp.zeros_like(tot)
        loop(chunks, steps)
        tot[chunks : chunks + 1, :] = jnp.sum(tot[0:chunks, :], axis=0, keepdims=True)
        eth[...] = two_part(jnp.exp2(tot[...]))
        loop(chunks, make_bc)

    if direct:
        work = SimpleNamespace(
            greet=greet, early=early, norm_own=norm_own, norm_edge=norm_edge, project=project, project_bc=project_bc
        )
        scalars = SimpleNamespace(adapter=lambda: adapter, seq_of=seq_of)
        late, end_front = front(r, dp, tp, dp_size, tp_size, load, scalars, work)
    else:
        early()
        norm_own()
        norm_edge()
        loop(BLOCKS, project)
        project_bc()
    decay = r.decay[0:1, :]

    def make_x(b):
        def part(c):
            window = px[b, pl.ds(pl.multiple_of(c * CHUNK + 8, 8), CHUNK + 8), :]
            u = conv(window, lambda j: small[b, j : j + 1, :], small[b, 4:5, :])
            s = sigmoid(u)
            x = u * s
            xs[b, rows(c), :] = x
            spx[b, rows(c), :] = (s + x * (1.0 - s)).astype(bf16)
            xdt = x * nn(dth[rows(c), :], expand[b])
            xd[b, rows(c), :] = xdt.astype(bf16)
            st[c, b] = nn(bt[c], (xdt * nn(tlh[rows(c), :], expand[b])).astype(bf16))
            z = gate[b, rows(c), :]
            s = sigmoid(z)
            g = z * s
            gate[b, rows(c), :] = g
            spz[b, rows(c), :] = (s + g * (1.0 - s)).astype(bf16)

        loop(chunks, part)
        et = nn(eth[...], expand[b])
        r.et[b] = et
        r.skips[b] = nn(r.skip[...], expand[b])
        total = st[0, b]
        for c in range(1, chunks):
            total = total * et[c : c + 1] + st[c, b]
        r.fresh[b] = total

    loop(BLOCKS, make_x)
    if direct:
        late.from_x()

    class Chain:
        def __init__(self, src, dst, ssem, rsem, to, place):
            self.src, self.dst, self.ssem, self.rsem, self.to, self.place = src, dst, ssem, rsem, to, place

        def copy(self, b):
            return remote(self.src.at[b], self.dst.at[b], self.ssem.at[b], self.rsem.at[b], (dp, self.to))

        def begin(self):
            @pl.when(self.place == 0)
            def _():
                for b in range(BLOCKS):
                    self.src[b] = r.fresh[b].astype(bf16)
                    self.copy(b).start()
                    self.dst[b] = jnp.zeros_like(self.dst[b])

        def step(self, cond):
            @pl.when(cond)
            def _():
                for b in range(BLOCKS):
                    self.copy(b).wait_recv()

                    @pl.when(self.place < tp_size - 1)
                    def _(b=b):
                        grown = self.dst[b].astype(f32) * r.et[b][chunks : chunks + 1]
                        self.src[b] = (grown + r.fresh[b]).astype(bf16)
                        self.copy(b).start()

        def end(self):
            @pl.when(self.place < tp_size - 1)
            def _():
                for b in range(BLOCKS):
                    self.copy(b).wait_send()

    at_first, at_last = tp == 0, tp == tp_size - 1
    s_chain = Chain(r.s_out, r.s_in, r.s_ss, r.s_rs, after, tp)
    r_chain = Chain(r.r_out, r.r_in, r.r_ss, r.r_rs, before, tp_size - 1 - tp)
    s_chain.begin()

    half = lax.broadcasted_iota(jnp.int32, (CHUNK, 128), 1) < 64

    def pair_terms(b, c, i):
        lanes = slice(128 * i, 128 * (i + 1))
        cum = r.cub[rows(c), :]
        cols = jnp.concatenate(
            [jnp.broadcast_to(cum[:, 2 * i + k : 2 * i + k + 1], (CHUNK, CHUNK)) for k in range(2)], axis=1
        )
        line = jnp.concatenate([cut[c, pl.ds(SLOT * b + 2 * i + k, 1), :] for k in range(2)], axis=1)
        mixing = jnp.exp2(jnp.minimum(cols - line, 0.0))
        scores = sc[c]
        weights = (mixing * jnp.concatenate([scores, scores], axis=1)).astype(bf16)
        pair = xd[b, rows(c), lanes]
        none = jnp.zeros_like(pair)
        split = jnp.concatenate([jnp.where(half, pair, none), jnp.where(half, none, pair)], axis=0)
        return lanes, mixing, weights, split

    def turn_heads(b):
        for c in range(chunks):
            r.cub[rows(c), :] = pltpu.roll(cu[rows(c), :], lax.rem(128 - SLOT * b, 128), 1)

    def inside(b):
        turn_heads(b)

        def part(c):
            for i in range(HEADS_B // 2):
                lanes, mixing, weights, split = pair_terms(b, c, i)
                y[b, rows(c), lanes] = nn(weights, split)

        loop(chunks, part)
        s_chain.step(jnp.logical_and(b == 0, tp == 1))

    loop(BLOCKS, inside)
    if direct:
        late.from_core()

    def back_out(b):
        gy[b] = small[b, 5:6, :] * (nn(gbr[...], wout[b]) + nn(ghid[...], r.odn[b]))

    loop(BLOCKS, back_out)
    for k in range(2, tp_size):
        s_chain.step(tp == k)

    ssq, crs = r.ssq, r.crs
    ssq[...] = jnp.zeros_like(ssq)
    crs[...] = jnp.zeros_like(crs)

    def gated(b, c):
        full = y[b, rows(c), :] + r.skips[b, 8:9, :] * xs[b, rows(c), :]
        return full, full * gate[b, rows(c), :]

    def carried(b):
        state = r.s_in[b].astype(f32)
        for c in range(chunks):
            added = st[c, b]
            st[c, b] = state
            grown = nn(cb[rows(c), :], state.astype(bf16))
            y[b, rows(c), :] = y[b, rows(c), :] + nn(ech[rows(c), :], expand[b]) * grown
            state = r.et[b, c : c + 1, :] * state + added
            _, act = gated(b, c)
            ssq[rows(c), :] = ssq[rows(c), :] + thirds(act * act)
            crs[rows(c), :] = crs[rows(c), :] + thirds(act * gy[b, rows(c), :])
        st[chunks, b] = state

    loop(BLOCKS, carried)
    inner = BLOCKS * WIDE

    def settle(c):
        inv = lax.rsqrt(jnp.sum(ssq[rows(c), :], axis=1, keepdims=True) / inner + EPSILON)
        cross = jnp.sum(crs[rows(c), :], axis=1, keepdims=True) / inner
        ssq[rows(c), :] = jnp.broadcast_to(inv, (CHUNK, 128))
        crs[rows(c), :] = jnp.broadcast_to(inv * inv * inv * cross, (CHUNK, 128))

    loop(chunks, settle)

    acc, nout, hout, hout_t = r.acc, r.nout, r.hout, r.hout_t

    def out_block(b):
        def part(c):
            full, act = gated(b, c)
            inv, slope = ssq[rows(c), 0:1], crs[rows(c), 0:1]
            nout[rows(c), :] = (act * inv * small[b, 5:6, :]).astype(bf16)
            g_gated = inv * gy[b, rows(c), :] - act * slope
            g_y = g_gated * gate[b, rows(c), :]
            gy[b, rows(c), :] = g_y
            gzx[b, rows(c), :WIDE] = (g_gated * full * spz[b, rows(c), :].astype(f32)).astype(bf16)
            rt[c, b] = nn(ct[c], (nn(ech[rows(c), :], expand[b]) * g_y).astype(bf16))

        loop(chunks, part)
        et = r.et[b]
        total = rt[chunks - 1, b]
        for c in range(chunks - 2, -1, -1):
            total = total * et[c : c + 1] + rt[c, b]
        r.fresh[b] = total
        r.odg[b] = nn(r.ghid_t[...], nout[...])
        part_b = nt(nout[...], wout[b])
        part_h = nt(nout[...], r.odn[b])
        part_t = nt(r.odn[b], nout[...])

        @pl.when(b == 0)
        def _():
            acc[...] = part_b
            hout[...] = part_h
            hout_t[...] = part_t

        @pl.when(b > 0)
        def _():
            acc[...] = acc[...] + part_b
            hout[...] = hout[...] + part_h
            hout_t[...] = hout_t[...] + part_t

    loop(BLOCKS, out_block)
    r_chain.begin()

    def write_out(c):
        branch = acc[rows(c), :] + nn(hout[rows(c), :].astype(bf16), r.oup[...])
        u = ext[rows(c, HALO), :].astype(f32)
        r.out_rows[rows(c), :] = (u + valid(c) * branch).astype(bf16)

    loop(chunks, write_out)
    oug = nn(hout_t[...].astype(bf16), gbr[...])
    r_chain.step(r_chain.place == 1)
    if direct:
        write_back = pltpu.make_async_copy(r.out_rows, r.out, r.own_sem.at[5])
        write_back.start()
        rest = Sums(r, dp, tp, dp_size, tp_size, 1)
        for k in range(2):
            pair = jnp.concatenate([r.odg[2 * k], r.odg[2 * k + 1]], axis=1)
            r.sum_out[1, k] = pair.astype(bf16)
        r.sum_out[1, 2] = oug.astype(bf16)
        r.sum_out[1, 3] = jnp.zeros((16, gbr.shape[1]), bf16)
        rest.start()
    else:
        r.oug[...] = oug

    dsc = r.dsc
    dsc[...] = jnp.zeros_like(dsc)

    def inside_back(b):
        turn_heads(b)

        def part(c):
            total = dsc[c]
            for i in range(HEADS_B // 2):
                lanes, mixing, weights, split = pair_terms(b, c, i)
                g = gy[b, rows(c), lanes].astype(bf16)
                both = nt(g, split) * mixing
                total = total + both[:, :CHUNK] + both[:, CHUNK:]
                back = tn(weights, g)
                xp[b, rows(c), lanes] = jnp.where(half, back[:CHUNK], back[CHUNK:])
            dsc[c] = total

        loop(chunks, part)
        r_chain.step(jnp.logical_and(b == 2, r_chain.place == 2))
        if direct:

            @pl.when(b == 1)
            def _():
                rest.middle()

    loop(BLOCKS, inside_back)
    for k in range(3, tp_size):
        r_chain.step(r_chain.place == k)
    if direct:
        rest.gathered()

    h1, h2, db, dc = r.h1, r.h2, r.db, r.dc
    for ref in (h1, h2, db, dc):
        ref[...] = jnp.zeros_like(ref)
    hs = r.hs
    hs[...] = jnp.zeros_like(hs)

    def head_sum(v, b):
        parts = two_part(v)
        sel = expand[b, :CHUNK, :]
        return nt(parts[:, :WIDE], sel) + nt(parts[:, WIDE:], sel)

    def carried_back(b, part):
        for c in part:
            state = (r.r_in[b].astype(f32) if c == chunks - 1 else r.fresh[b])
            low = state.astype(bf16)
            meet = jnp.broadcast_to(jnp.sum(state * st[c + 1, b], axis=0, keepdims=True), (8, WIDE))
            hs[c] = hs[c] + head_sum(meet, b)
            tail = nn(tlh[rows(c), :], expand[b])
            grow = nn(ech[rows(c), :], expand[b])
            dt = nn(dth[rows(c), :], expand[b])
            x, g = xs[b, rows(c), :], gy[b, rows(c), :]
            back = xp[b, rows(c), :] + tail * nn(bb[rows(c), :], low)
            xdt = x * dt
            h1[rows(c), :] = h1[rows(c), :] + head_sum(g * y[b, rows(c), :] - xdt * back, b)
            h2[rows(c), :] = h2[rows(c), :] + head_sum(x * back, b)
            dc[rows(c), :] = dc[rows(c), :] + nt((grow * g).astype(bf16), st[c, b].astype(bf16))
            db[rows(c), :] = db[rows(c), :] + nt((tail * xdt).astype(bf16), low)
            px[b, rows(c), :] = (dt * back + r.skips[b, 8:9, :] * g) * spx[b, rows(c), :].astype(f32)
            r.fresh[b] = r.et[b, c : c + 1, :] * state + rt[c, b]

    up_tri = jnp.where(
        lax.broadcasted_iota(jnp.int32, (CHUNK, CHUNK), 0) <= lax.broadcasted_iota(jnp.int32, (CHUNK, CHUNK), 1),
        1.0,
        0.0,
    ).astype(f32)
    gdt = r.gdt

    def finish_bc(c):
        low = jnp.where(low_tri, dsc[c], 0.0).astype(bf16)
        d_c = dc[rows(c), :] + nn(low, bb[rows(c), :])
        d_b = db[rows(c), :] + tn(low, cb[rows(c), :])
        u = ub[rows(c), :]
        s = sigmoid(u)
        pb[rows(c), :] = jnp.concatenate([d_b, d_c], axis=1) * (s + u * s * (1.0 - s))
        da = jnp.dot(up_tri, h1[rows(c), :], precision=HIGHEST, preferred_element_type=f32) + hs[c, 0:1, :]
        gdt[rows(c), :] = ((h2[rows(c), :] + decay * da) * sigmoid(pd[rows(c), :])).astype(bf16)

    def edges():
        return [
            remote(r.ex_out, r.ex_in, r.e_ss.at[0], r.e_rs.at[0], (dp, before)),
            remote(r.eb_out, r.eb_in, r.e_ss.at[1], r.e_rs.at[1], (dp, before)),
        ]

    def send_edges():
        @pl.when(jnp.logical_not(at_first))
        def _():
            for b in range(BLOCKS):
                r.ex_out[b] = px[b, 0:8, :]
            r.eb_out[...] = pb[0:8, :]
            for copy in edges():
                copy.start()

    def take_edges():
        @pl.when(jnp.logical_not(at_last))
        def _():
            for copy in edges():
                copy.wait_recv()
            for b in range(BLOCKS):
                px[b, rows_n : rows_n + 8, :] = r.ex_in[b]
            pb[rows_n : rows_n + 8, :] = r.eb_in[...]

        @pl.when(at_last)
        def _():
            for b in range(BLOCKS):
                px[b, rows_n : rows_n + 8, :] = jnp.zeros((8, WIDE), f32)
            pb[rows_n : rows_n + 8, :] = jnp.zeros((8, 256), f32)

    def conv_back(window, kernel_row):
        size = window.shape[0] - 8
        total = kernel_row(3) * window[:size]
        for j in range(3):
            shifted = pltpu.roll(window, window.shape[0] - (3 - j), 0)
            total = total + kernel_row(j) * shifted[:size]
        return total

    if direct:
        returns = Returns(r, dp, tp, dp_size)

    def finish_rows(at, size):
        here = slice(at, at + size)
        gbc = conv_back(pb[at : at + size + 8, :], lambda j: bc_kernel[j : j + 1, :]).astype(bf16)
        acc[here, :] = nt(gbc, r.wbc[...]) + nt(gdt[here, :], r.wdt[...])
        hout[here, :] = jnp.zeros((size, 16), f32)

        def in_block(b):
            g = conv_back(px[b, at : at + size + 8, :], lambda j: small[b, j : j + 1, :]).astype(bf16)
            gzx[b, here, WIDE:] = g
            both = gzx[b, here, :]
            acc[here, :] = acc[here, :] + nt(both, zx[b])
            hout[here, :] = hout[here, :] + nt(both, up[b])

        loop(BLOCKS, in_block)
        g = acc[here, :] + nn(hout[here, :].astype(bf16), r.idn[...])
        u = ext[at + HALO : at + HALO + size, :].astype(f32)
        inv = lax.rsqrt(jnp.mean(u * u, axis=1, keepdims=True) + EPSILON)
        v = r.gain[...].astype(f32)[None] * g
        cross = jnp.mean(v * u, axis=1, keepdims=True)
        r.tg[here, :] = (cot[here, :].astype(f32) + inv * v - u * (inv * inv * inv * cross)).astype(bf16)
        if direct:
            for d in range(at // returns.block, (at + size) // returns.block):
                returns.send(d)

    upper = range(chunks - 1, chunks // 2 - 1, -1)
    lower = range(chunks // 2 - 1, -1, -1)
    loop(BLOCKS, lambda b: carried_back(b, upper))
    for c in upper:
        finish_bc(c)
    middle = rows_n // 2
    finish_rows(middle, middle - 64)
    if direct:
        rest.pass_on()
    loop(BLOCKS, lambda b: carried_back(b, lower))
    for c in lower:
        finish_bc(c)
    send_edges()
    finish_rows(0, middle)
    take_edges()
    finish_rows(rows_n - 64, 64)

    hid_t = nt(r.idn[...], nrm[HALO:, :]).astype(bf16)
    ghin_t = hout_t
    ghin_t[...] = jnp.zeros_like(ghin_t)

    def adapter_grads(b):
        g = gzx[b]
        ghin_t[...] = ghin_t[...] + nt(up[b], g)
        iug = nn(hid_t, g)
        if direct:
            r.sum_out[0, b] = iug.astype(bf16)
        else:
            r.iug[b] = iug

    loop(BLOCKS, adapter_grads)
    idg = nn(ghin_t[...].astype(bf16), nrm[HALO:, :])
    if direct:
        ups = Sums(r, dp, tp, dp_size, tp_size, 0)
        ups.start()
        ends = Toward(
            tp,
            tp_size,
            lambda t: (dp, t),
            lambda t: r.end_out,
            lambda t: r.end_in.at[t],
            r.ge_ss,
            r.ge_rs,
        )
        r.end_out[...] = idg.astype(bf16)
        ends.start()
        r.end_in[tp] = r.end_out[...]
        ups.middle()
        ends.wait()
        total = r.end_in[0].astype(f32)
        for t in range(1, BLOCKS):
            total = total + r.end_in[t].astype(f32)
        r.end_all[...] = total.astype(bf16)
        spread = Toward(
            dp,
            dp_size,
            lambda d: (d, tp),
            lambda d: r.end_all,
            lambda d: r.all_end.at[d],
            r.gf_ss,
            r.gf_rs,
        )
        spread.start()
        own_end = pltpu.make_async_copy(r.end_all, r.all_end.at[dp], r.own_sem.at[6])
        own_end.start()
        ups.gathered()
        spread.wait()
        own_end.wait()
        returns.finish()
        rest.finish()
        ups.finish()
        ends.finish()
        spread.finish()
        write_back.wait()
        end_front()
    else:
        r.idg[...] = idg
    s_chain.end()
    r_chain.end()

    @pl.when(jnp.logical_not(at_first))
    def _():
        for copy in edges():
            copy.wait_send()


def settle_kernel(dealt, adapters, out, tg, ups, rest, ends, o_out, o_tok, o_idg, o_iug, o_odg, o_oug, *scratch):
    v_out, v_tg, v_ups, v_rest, v_ends, s_idg, s_iug, s_odg, s_oug, sems = scratch
    count = dealt.shape[0]
    loads = [
        pltpu.make_async_copy(src, dst, sems.at[i])
        for i, (src, dst) in enumerate(((out, v_out), (tg, v_tg), (ups, v_ups), (rest, v_rest), (ends, v_ends)))
    ]
    for copy in loads:
        copy.start()
    for ref in (s_idg, s_iug, s_odg, s_oug):
        ref[...] = jnp.zeros_like(ref)
    loads[0].wait()
    stores = [pltpu.make_async_copy(v_out, o_out, sems.at[5])]
    stores[0].start()
    loads[1].wait()
    for s in range(count):
        stores.append(pltpu.make_async_copy(v_tg.at[dealt[s]], o_tok.at[s], sems.at[6 + s]))
        stores[-1].start()
    for copy in loads[2:]:
        copy.wait()
    half = 2 * WIDE
    for s in range(count):
        k, g = adapters[s], dealt[s]
        s_idg[k] = s_idg[k] + v_ends[g].astype(f32)
        for i in range(2):
            s_iug[k, :, i, :] = s_iug[k, :, i, :] + v_ups[g, :, i * WIDE : (i + 1) * WIDE].astype(f32)
            s_odg[k, :, i * half : (i + 1) * half] = s_odg[k, :, i * half : (i + 1) * half] + v_rest[i, g].astype(f32)
        s_oug[k] = s_oug[k] + v_rest[2, g].astype(f32)
    for i, (src, dst) in enumerate(((s_idg, o_idg), (s_iug, o_iug), (s_odg, o_odg), (s_oug, o_oug))):
        stores.append(pltpu.make_async_copy(src, dst, sems.at[6 + count + i]))
        stores[-1].start()
    for copy in stores:
        copy.wait()


def settle_call(dealt, adapters, res):
    n, block, d = res.tg_in.shape
    smem, any_space = pl.BlockSpec(memory_space=pltpu.SMEM), pl.BlockSpec(memory_space=pl.ANY)
    grads = [
        jax.ShapeDtypeStruct((ADAPTERS, 16, d), f32),
        jax.ShapeDtypeStruct((ADAPTERS, 16, 2, WIDE), f32),
        jax.ShapeDtypeStruct((ADAPTERS, 16, BLOCKS * WIDE), f32),
        jax.ShapeDtypeStruct((ADAPTERS, 16, d), f32),
    ]
    gathered = (res.out, res.tg_in, res.all_up, res.all_rest, res.all_end)
    return pl.pallas_call(
        settle_kernel,
        out_shape=[
            jax.ShapeDtypeStruct(res.out.shape, bf16),
            jax.ShapeDtypeStruct((n, block, d), bf16),
        ]
        + grads,
        in_specs=[smem] * 2 + [any_space] * 5,
        out_specs=[any_space] * 6,
        scratch_shapes=[pltpu.VMEM(v.shape, v.dtype) for v in gathered]
        + [pltpu.VMEM(v.shape, v.dtype) for v in grads]
        + [pltpu.SemaphoreType.DMA((10 + n,))],
    )(dealt, adapters, *gathered)


def mixer_call(direct, scalars, arrays):
    rows_n = arrays["cot"].shape[0]
    chunks = rows_n // CHUNK
    d = arrays["cot"].shape[1]
    outs = dict(
        out=((rows_n, d), bf16),
        tg=((rows_n, d), bf16),
        idg=((16, d), f32),
        iug=((BLOCKS, 16, 2 * WIDE), f32),
        odg=((BLOCKS, 16, WIDE), f32),
        oug=((16, d), f32),)
    wide = (BLOCKS, rows_n, WIDE)
    state = (BLOCKS, 128, WIDE)
    scratch = dict(
        idn=((16, d), bf16),
        oup=((16, d), bf16),
        odn=((BLOCKS, 16, WIDE), bf16),
        expand=((BLOCKS, 256, WIDE), bf16),
        skip=((16, 256), bf16),
        decay=((8, 128), f32),
        ghid_t=((16, rows_n), bf16),
        skips=((BLOCKS, 16, WIDE), f32),
        nrm=((rows_n + HALO, d), bf16),
        hid=((rows_n + HALO, 16), bf16),
        gate=(wide, f32),
        spz=(wide, bf16),
        px=((BLOCKS, rows_n + HALO, WIDE), f32),
        xs=(wide, f32),
        spx=(wide, bf16),
        xd=(wide, bf16),
        pb=((rows_n + HALO, 256), f32),
        pd=((rows_n, 128), f32),
        dth=((rows_n, 256), bf16),
        ech=((rows_n, 256), bf16),
        tlh=((rows_n, 256), bf16),
        eth=((16, 256), bf16),
        et=((BLOCKS, 16, WIDE), f32),
        cu=((rows_n, 128), f32),
        cub=((rows_n, 128), f32),
        cut=((chunks, 128, 128), f32),
        tot=((16, 128), f32),
        ub=((rows_n, 256), f32),
        bb=((rows_n, 128), bf16),
        cb=((rows_n, 128), bf16),
        bt=((chunks, 128, 128), bf16),
        ct=((chunks, 128, 128), bf16),
        sc=((chunks, 128, 128), f32),
        st=((chunks + 1,) + state, f32),
        rt=((chunks,) + state, f32),
        fresh=(state, f32),
        s_in=(state, bf16),
        s_out=(state, bf16),
        r_in=(state, bf16),
        r_out=(state, bf16),
        y=(wide, f32),
        gy=(wide, f32),
        gzx=((BLOCKS, rows_n, 2 * WIDE), bf16),
        gbr=((rows_n, d), bf16),
        ghid=((rows_n, 16), bf16),
        ssq=((rows_n, 128), f32),
        crs=((rows_n, 128), f32),
        acc=((rows_n, d), f32),
        nout=((rows_n, WIDE), bf16),
        hout=((rows_n, 16), f32),
        hout_t=((16, rows_n), f32),
        dsc=((chunks, 128, 128), f32),
        h1=((rows_n, 128), f32),
        h2=((rows_n, 128), f32),
        db=((rows_n, 128), f32),
        dc=((rows_n, 128), f32),
        hs=((chunks, 8, 128), f32),
        gdt=((rows_n, 128), bf16),
        ex_out=((BLOCKS, 8, WIDE), f32),
        ex_in=((BLOCKS, 8, WIDE), f32),
        eb_out=((8, 256), f32),
        eb_in=((8, 256), f32),)
    sems = dict(s_ss=(BLOCKS,), s_rs=(BLOCKS,), r_ss=(BLOCKS,), r_rs=(BLOCKS,), e_ss=(2,), e_rs=(2,))
    if direct:
        n, block = arrays["tokens"].shape[:2]
        scratch.update(iug=outs["iug"], odg=outs["odg"])
        outs = dict(
            out=((rows_n, d), bf16),
            tg_in=((n, block, d), bf16),
            all_up=((n, 16, d), bf16),
            all_rest=((BLOCKS, n, 16, d), bf16),
            all_end=((n, 16, d), bf16),
        )
        scratch.update(
            out_rows=((rows_n, d), bf16),
            tok_out=((n, block, d), bf16),
            ext=((rows_n + HALO, d), bf16),
            zx=((BLOCKS, d, 2 * WIDE), bf16),
            wout=((BLOCKS, d, WIDE), bf16),
            wbc=((d, 256), bf16),
            dts=((BLOCKS, n, 16, 128), bf16),
            wdt=((d, 128), bf16),
            up=((BLOCKS, 16, 2 * WIDE), bf16),
            small=((BLOCKS, 16, WIDE), f32),
            sum_out=((2, BLOCKS, 16, d), bf16),
            sum_in=((2, BLOCKS, 16, d), bf16),
            sum_all=((2, 16, d), bf16),
            end_out=((16, d), bf16),
            end_in=((BLOCKS, 16, d), bf16),
            end_all=((16, d), bf16),
        )
        for name in LOADED:
            scratch["v_" + name] = (arrays[name].shape, arrays[name].dtype)
        pairs = dict(zx=(6, n), wo=(6, n), bc=(3, n), tok=(n,), dt=(n,), d2=(BLOCKS,), up=(BLOCKS,), sm=(BLOCKS,))
        pairs.update(ha=(1,), tg=(n,), ga=(BLOCKS,), gb=(BLOCKS,), gc=(n,), gd=(n,), g3=(BLOCKS,))
        pairs.update(ge=(BLOCKS,), gf=(n,))
        for name, shape in pairs.items():
            sems[name + "_ss"] = shape
            sems[name + "_rs"] = (BLOCKS, n) if name in ("zx", "wo") else shape[-1:]
        sems.update(own_sem=(7,), load_sem=(len(LOADED),))
    names = list(scalars) + list(arrays) + list(outs) + list(scratch) + list(sems)
    smem = pl.BlockSpec(memory_space=pltpu.SMEM)
    vmem = pl.BlockSpec(memory_space=pl.ANY if direct else pltpu.VMEM)
    results = pl.pallas_call(
        partial(mixer_kernel, direct, names),
        out_shape=[jax.ShapeDtypeStruct(*v) for v in outs.values()],
        in_specs=[smem] * len(scalars) + [vmem] * len(arrays),
        out_specs=[vmem] * len(outs),
        scratch_shapes=[pltpu.VMEM(*v) for v in scratch.values()]
        + [pltpu.SemaphoreType.DMA(n) for n in sems.values()],
        compiler_params=pltpu.CompilerParams(
            collective_id=1, has_side_effects=True, vmem_limit_bytes=63 * 1024 * 1024
        ),
    )(*scalars.values(), *arrays.values())
    return SimpleNamespace(**dict(zip(outs, results)))


def pack_small(x_kernel, x_offset, out_gain, dt_bias, a_log, d_skip):
    def block(v):
        return v.reshape(-1, BLOCKS, v.shape[-1] // BLOCKS).transpose(1, 0, 2)

    def heads(v):
        return jnp.pad(block(v[None]), ((0, 0), (0, 0), (0, WIDE - HEADS_B)))

    parts = [
        block(x_kernel),
        block(x_offset[None]),
        block(out_gain.astype(f32)[None]),
        heads(dt_bias),
        heads(a_log),
        heads(d_skip),
        jnp.zeros((BLOCKS, 7, WIDE), f32),
    ]
    return jnp.concatenate(parts, axis=1)


def shards(
    tokens,
    cotangent,
    lengths,
    dealt_to,
    adapter_id,
    norm_gain,
    w_zx,
    w_dt,
    w_bc,
    x_kernel,
    x_offset,
    bc_kernel,
    bc_offset,
    dt_bias,
    a_log,
    d_skip,
    out_gain,
    w_out,
    inlet_down,
    inlet_up,
    outlet_down,
    outlet_up,
):
    d = tokens.shape[3]
    tp_size, dp_size = lax.axis_size("tensor"), lax.axis_size("dp")
    if tp_size == BLOCKS and dp_size % 2 == 0 and w_bc.shape[0] % 16 == 0 and tokens.shape[2] * 2 <= CHUNK:
        n, block = tokens.shape[0], tokens.shape[2]
        res = mixer_call(
            True,
            dict(lengths=lengths, dealt_to=dealt_to, adapter_id=adapter_id),
            dict(
                tokens=tokens.reshape(n, block, d),
                cot=cotangent.reshape(-1, d),
                gain=norm_gain,
                w_zx=w_zx,
                w_out=w_out.T,
                w_bc=w_bc,
                w_dt_in=w_dt.T,
                x_kernel=x_kernel,
                x_offset=x_offset,
                out_gain=out_gain,
                dt_bias=dt_bias,
                a_log=a_log,
                d_skip=d_skip,
                bc_kernel=bc_kernel,
                bc_offset=bc_offset,
                inlet_down=inlet_down.transpose(0, 2, 1),
                inlet_up=inlet_up,
                outlet_down=outlet_down.transpose(0, 2, 1),
                outlet_up=outlet_up,
            ),
        )
        out, tok, idg, iug, odg, oug = settle_call(dealt_to, adapter_id, res)
        return (
            out.reshape(1, -1, d),
            tok.reshape(tokens.shape),
            idg.transpose(0, 2, 1),
            iug,
            odg.transpose(0, 2, 1),
            oug,
        )
    group_id, place = lax.axis_index("dp"), lax.axis_index("tensor")
    seq_count = dealt_to.shape[0]
    slots = jnp.arange(seq_count, dtype=jnp.int32)
    seq_of = jnp.sum((dealt_to[None, :] == slots[:, None]).astype(jnp.int32) * slots[None, :], axis=1)
    own = jnp.take(seq_of, group_id)
    adapter = jnp.take(adapter_id, own)
    chosen = (jnp.arange(inlet_down.shape[0], dtype=jnp.int32) == adapter).astype(f32)

    picked = jnp.take(tokens, seq_of, axis=0)
    tok = lax.all_to_all(picked, "dp", split_axis=0, concat_axis=2, tiled=True).reshape(-1, d)
    rows_n = tok.shape[0]
    ends = lax.ppermute(tok[-HALO:], "tensor", [(i, i + 1) for i in range(tp_size - 1)])
    ext = jnp.concatenate([ends, tok], axis=0)

    def both(v, axis_dp, axis_tp):
        v = lax.all_gather(v, "dp", axis=axis_dp, tiled=True)
        return lax.all_gather(v, "tensor", axis=axis_tp, tiled=True)

    full_zx = both(w_zx, 0, 2)
    full_out = both(w_out, 1, 0)
    full_dt = both(w_dt, 0, 1)
    full_bc = lax.all_gather(w_bc, "dp", axis=0, tiled=True)
    zx = full_zx.reshape(d, 2, BLOCKS, WIDE).transpose(2, 0, 1, 3).reshape(BLOCKS, d, 2 * WIDE)
    wout = full_out.T.reshape(d, BLOCKS, WIDE).transpose(1, 0, 2)
    wdt = jnp.pad(full_dt.reshape(d, BLOCKS, HEADS_B), ((0, 0), (0, 0), (0, SLOT - HEADS_B))).reshape(d, BLOCKS * SLOT)
    wdt = jnp.pad(wdt, ((0, 0), (0, 128 - BLOCKS * SLOT)))

    def over_tp(v):
        return lax.all_gather(v, "tensor", axis=v.ndim - 1, tiled=True)

    small = pack_small(*(over_tp(v) for v in (x_kernel, x_offset, out_gain, dt_bias, a_log, d_skip)))
    up = over_tp(jnp.take(inlet_up, adapter, axis=0))
    up = up.reshape(16, 2, BLOCKS, WIDE).transpose(2, 0, 1, 3).reshape(BLOCKS, 16, 2 * WIDE)

    res = mixer_call(
        False,
        dict(lengths=lengths, dealt_to=dealt_to, adapter_id=adapter_id),
        dict(
            ext=ext,
            cot=cotangent.reshape(rows_n, d),
            gain=norm_gain,
            zx=zx,
            wout=wout,
            wbc=full_bc,
            wdt=wdt,
            small=small,
            up=up,
            bc_kernel=bc_kernel,
            bc_offset=bc_offset,
            inlet_down=inlet_down.transpose(0, 2, 1),
            outlet_down=outlet_down.transpose(0, 2, 1),
            outlet_up=outlet_up,
        ),
    )
    output = res.out.reshape(1, rows_n, d)
    returned = lax.all_to_all(res.tg.reshape(1, 1, rows_n, d), "dp", split_axis=2, concat_axis=0, tiled=True)
    token_grads = jnp.take(returned, dealt_to, axis=0)
    pick = chosen[:, None, None]
    odg = res.odg.transpose(1, 0, 2).reshape(16, BLOCKS * WIDE)
    idg, odg, oug = lax.psum((pick * res.idg[None], pick * odg[None], pick * res.oug[None]), ("dp", "tensor"))
    iug = res.iug.reshape(BLOCKS, 16, 2, WIDE).transpose(1, 2, 0, 3).reshape(16, 2, BLOCKS * WIDE)
    iug = lax.psum_scatter(iug, "tensor", scatter_dimension=2, tiled=True)
    iug = lax.psum(pick[..., None] * iug[None], "dp")
    return (output, token_grads, idg.transpose(0, 2, 1), iug, odg.transpose(0, 2, 1), oug)


def solution(mesh):
    in_specs = (
        P(None, "tensor", "dp", None),
        P("dp", "tensor", None),
        P(),
        P(),
        P(),
        P(),
        P("dp", None, "tensor"),
        P("dp", "tensor"),
        P("dp", None),
        P(None, "tensor"),
        P("tensor"),
        P(),
        P(),
        P("tensor"),
        P("tensor"),
        P("tensor"),
        P("tensor"),
        P("tensor", "dp"),
        P(),
        P(None, None, None, "tensor"),
        P(),
        P(),
    )
    out_specs = (
        P("dp", "tensor", None),
        P(None, "tensor", "dp", None),
        P(),
        P(None, None, None, "tensor"),
        P(),
        P(),
    )
    return jax.shard_map(shards, mesh=mesh, in_specs=in_specs, out_specs=out_specs, check_vma=False)
```

time: 792 us -> 155 us (0.20)
  waiting for transfers between devices: 344 us -> 0 us
  matrix products: 158 us -> 0 us
  Pallas kernels: 0 us -> 154 us
  blocking collectives: 113 us -> 0 us
  local copies, waits for them, and re-layouts: 83.5 us -> 0 us
  other arithmetic: 56.7 us -> 0 us
  between operations: 18 us -> 0.81 us
  starting transfers between devices: 13.7 us -> 0 us
    psum x2 -> x0, waiting for transfers between devices: 205 us -> none  [the longest x1 134 us: shards(): lax.psum((chosen[:, None, None] * indown_sum[None], chosen[:, None, None]...]
    dot_general x43 -> x0, matrix products: 158 us -> none  [the longest x3 54.3 us: state_mixer(): inside = jnp.einsum('ctsh,cshp->cthp', weights, block_x, precision=HIGHEST)]
    pallas_call x0 -> x2, Pallas kernels: none -> 154 us  [the longest x1 150 us: mixer_call(): pl.pallas_call(partial(mixer_kernel, direct, names), out_shape=[jax.Shape...]
    reduce_scatter x5 -> x0, waiting for transfers between devices: 112 us -> none  [the longest x1 58.3 us: shards(): lax.psum_scatter(jnp.dot(normed_out, full_out, preferred_element_type=jnp...]
    all_gather x5 -> x0, blocking collectives: 101 us -> none  [the longest x1 31.6 us: shards(): lax.all_gather(w_out, 'dp', axis=1, tiled=True)]
    unnamed x223 -> x0, local copies, waits for them, and re-layouts: 36.8 us -> none
    all_to_all x2 -> x0, waiting for transfers between devices: 26.5 us -> none  [the longest x1 26.5 us: shards(): lax.all_to_all(picked, 'dp', split_axis=0, concat_axis=2, tiled=True)]
    mul x9 -> x0, other arithmetic: 15 us -> none  [the longest x4 5.24 us: causal_conv(): running = running + kernel[offset][None, :] * padded[offset:offset + length]]
  transfers between devices with their start and end apart: 12 -> 0, of which waited for: 6 -> 0; matrix products, arithmetic and copies ran while one was open for 14% -> 0% of each run, Pallas kernels for 0% -> 0%
where the time goes in v1:
time: 155 us
  Pallas kernels  154 us (99%)
    pallas_call x1, Pallas kernels, mixer_call(): pl.pallas_call(partial(mixer_kernel, direct, names), out_shape=[jax.Shape...  150 us
    pallas_call x1, Pallas kernels, settle_call(): pl.pallas_call(settle_kernel, out_shape=[jax.ShapeDtypeStruct(res.out.sha...  4.11 us

profile of v1, /device:TPU:0, one launch (start us, length us, event | category | flops | bytes accessed | tf_op | source)
XLA Modules:
  0.0 155.3 jit_solution(1753109276562051286)
XLA Ops:
  0.6 150.3 %shard_map.253 = (bf16[512,768]{1,0:T(8,128)(2,1)}, bf16[8,64,768]{2,1,0:T(8,128)(2,1)}, bf16[8,16,768]{2,1,0:T(8,128)(2,1)}, bf16[4,8,16,768]{3,2,1,0:T(8,128)(2,1)}, bf16[8,16,768]{2,1,0:T(8,128)(2,1)}) custom-call(s32[8]{0:T(128)} %refs_0_.1, s32[8]{0:T(128)} %dealt.1, s32[8]{0:T(128)} %adapters.1, bf16[8,64,768]{2,1,0:T(8,128)(2,1)} %bitcast.12, ...), custom_call_target="tpu_custom_call" | custom-call | tf_op jit(solution)/shard_map/pallas_call | solution.py:1271
  151.0 4.1 %shard_map.254 = (bf16[512,768]{1,0:T(8,128)(2,1)}, bf16[8,64,768]{2,1,0:T(8,128)(2,1)}, f32[8,16,768]{2,1,0:T(8,128)}, f32[8,16,2,384]{3,2,1,0:T(2,128)}, f32[8...) custom-call(s32[8]{0:T(128)} %dealt.1, s32[8]{0:T(128)} %adapters.1, bf16[512,768]{1,0:T(8,128)(2,1)} %get-tuple-element.17.out, ...), custom_call_target="tpu_custom_call" | custom-call | tf_op jit(solution)/shard_map/pallas_call | solution.py:1139

commit v2 on v1

--- a/solution.py
+++ b/solution.py
@@ -68,8 +68,8 @@
     return v[:, :128] + v[:, 128:256] + v[:, 256:384]
 
 
-def loop(count, body):
-    lax.fori_loop(0, count, lambda i, carry: (body(i), carry)[1], 0)
+def loop(count, body, unroll=1):
+    lax.fori_loop(0, count, lambda i, carry: (body(i), carry)[1], 0, unroll=unroll)
 
 
 def remote(src, dst, ssem, rsem, peer):
@@ -313,7 +313,6 @@
     zx.own_done()
     wbc.from_y(zx.nz - 1)
     own_out.wait()
-    wout.begin()
     work.early()
     dts2.wait()
     ups.wait()
@@ -347,19 +346,14 @@
     work.norm_edge()
     work.project(tp)
     zx.from_x()
-    wout.hop(1)
-    wout.from_y(0)
+    wout.begin()
     zx.column(zx.core).wait_recv()
     work.project(zx.core)
     work.project_bc()
-    wout.hop(2)
-    wout.from_y(1)
     work.project(zx.far)
+    wout.hop(1)
+    wout.from_y(0)
     zx.from_far_core()
-    wout.hop(3)
-    wout.from_y(2)
-    wout.from_y(3)
-    wout.own_done()
     work.project(zx.far_core)
 
     def end():
@@ -533,7 +527,7 @@
     ext, nrm, hid, zx, up = r.ext, r.nrm, r.hid, r.zx, r.up
     gate, spz, px, xs, spx, xd = r.gate, r.spz, r.px, r.xs, r.spx, r.xd
     expand, small, pb, pd = r.expand, r.small, r.pb, r.pd
-    dth, ech, tlh, eth, cu, cut, tot = r.dth, r.ech, r.tlh, r.eth, r.cu, r.cut, r.tot
+    eth, cu, cut, tot = r.eth, r.cu, r.cut, r.tot
     ub, bb, cb, bt, ct, sc = r.ub, r.bb, r.cb, r.bt, r.ct, r.sc
     st, rt, y, gy, gzx, xp = r.st, r.rt, r.y, r.gy, r.gzx, r.px
 
@@ -567,7 +561,6 @@
         loop(BLOCKS, fill_expand)
         loop(chunks, mask_cot)
         ghid[...] = nt(gbr[...], r.oup[...]).astype(bf16)
-        r.ghid_t[...] = nt(r.oup[...], gbr[...]).astype(bf16)
 
     def norm_rows(at, size):
         u = ext[pl.ds(at, size), :].astype(f32)
@@ -608,9 +601,9 @@
         cu[rows(c), :] = cum
         cut[c] = cum.T
         tot[pl.ds(c, 1), :] = total
-        dth[rows(c), :] = two_part(dt)
-        ech[rows(c), :] = two_part(jnp.exp2(cum))
-        tlh[rows(c), :] = two_part(jnp.exp2(total - cum))
+        r.rates[c, 0:CHUNK, :] = two_part(jnp.exp2(cum))
+        r.rates[c, CHUNK : 2 * CHUNK, :] = two_part(dt)
+        r.rates[c, 2 * CHUNK :, :] = two_part(jnp.exp2(total - cum))
 
     bc_kernel, bc_offset = r.bc_kernel, r.bc_offset
 
@@ -659,6 +652,60 @@
         project_bc()
     decay = r.decay[0:1, :]
 
+    class Chain:
+        def __init__(self, src, dst, ssem, rsem, to, place):
+            self.src, self.dst, self.ssem, self.rsem, self.to, self.place = src, dst, ssem, rsem, to, place
+
+        def copy(self, b):
+            return remote(self.src.at[b], self.dst.at[b], self.ssem.at[b], self.rsem.at[b], (dp, self.to))
+
+        def begin(self, b):
+            @pl.when(self.place == 0)
+            def _():
+                self.src[b] = r.fresh[b].astype(bf16)
+                self.copy(b).start()
+                self.dst[b] = jnp.zeros_like(self.dst[b])
+
+        def step(self, cond, b):
+            @pl.when(cond)
+            def _():
+                self.copy(b).wait_recv()
+
+                @pl.when(self.place < tp_size - 1)
+                def _():
+                    grown = self.dst[b].astype(f32) * r.et[b][chunks : chunks + 1]
+                    self.src[b] = (grown + r.fresh[b]).astype(bf16)
+                    self.copy(b).start()
+
+        def within(self, b):
+            self.begin(b)
+            for place, lag in ((1, 1), (2, 3)):
+                self.step(jnp.logical_and(self.place == place, b >= lag), jnp.maximum(b - lag, 0))
+
+        def after_first(self):
+            self.step(self.place == 1, BLOCKS - 1)
+
+        def between(self, b):
+            @pl.when(b == 2)
+            def _():
+                for k in range(BLOCKS - 3, BLOCKS):
+                    self.step(self.place == 2, k)
+
+        def rest(self):
+            for place in range(3, tp_size):
+                for b in range(BLOCKS):
+                    self.step(self.place == place, b)
+
+        def end(self):
+            @pl.when(self.place < tp_size - 1)
+            def _():
+                for b in range(BLOCKS):
+                    self.copy(b).wait_send()
+
+    at_first, at_last = tp == 0, tp == tp_size - 1
+    s_chain = Chain(r.s_out, r.s_in, r.s_ss, r.s_rs, after, tp)
+    r_chain = Chain(r.r_out, r.r_in, r.r_ss, r.r_rs, before, tp_size - 1 - tp)
+
     def make_x(b):
         def part(c):
             window = px[b, pl.ds(pl.multiple_of(c * CHUNK + 8, 8), CHUNK + 8), :]
@@ -667,16 +714,17 @@
             x = u * s
             xs[b, rows(c), :] = x
             spx[b, rows(c), :] = (s + x * (1.0 - s)).astype(bf16)
-            xdt = x * nn(dth[rows(c), :], expand[b])
+            wide = nn(r.rates[c, CHUNK:, :], expand[b])
+            xdt = x * wide[:CHUNK]
             xd[b, rows(c), :] = xdt.astype(bf16)
-            st[c, b] = nn(bt[c], (xdt * nn(tlh[rows(c), :], expand[b])).astype(bf16))
+            st[c, b] = nn(bt[c], (xdt * wide[CHUNK:]).astype(bf16))
             z = gate[b, rows(c), :]
             s = sigmoid(z)
             g = z * s
             gate[b, rows(c), :] = g
             spz[b, rows(c), :] = (s + g * (1.0 - s)).astype(bf16)
 
-        loop(chunks, part)
+        loop(chunks, part, chunks)
         et = nn(eth[...], expand[b])
         r.et[b] = et
         r.skips[b] = nn(r.skip[...], expand[b])
@@ -684,48 +732,26 @@
         for c in range(1, chunks):
             total = total * et[c : c + 1] + st[c, b]
         r.fresh[b] = total
+        s_chain.within(b)
+        if direct:
+
+            @pl.when(b == 0)
+            def _():
+                late.hop(2)
+                late.from_y(1)
+
+            @pl.when(b == 1)
+            def _():
+                late.hop(3)
+                late.from_y(2)
+
+            @pl.when(b == 2)
+            def _():
+                late.from_y(3)
+                late.own_done()
 
     loop(BLOCKS, make_x)
-    if direct:
-        late.from_x()
-
-    class Chain:
-        def __init__(self, src, dst, ssem, rsem, to, place):
-            self.src, self.dst, self.ssem, self.rsem, self.to, self.place = src, dst, ssem, rsem, to, place
-
-        def copy(self, b):
-            return remote(self.src.at[b], self.dst.at[b], self.ssem.at[b], self.rsem.at[b], (dp, self.to))
-
-        def begin(self):
-            @pl.when(self.place == 0)
-            def _():
-                for b in range(BLOCKS):
-                    self.src[b] = r.fresh[b].astype(bf16)
-                    self.copy(b).start()
-                    self.dst[b] = jnp.zeros_like(self.dst[b])
-
-        def step(self, cond):
-            @pl.when(cond)
-            def _():
-                for b in range(BLOCKS):
-                    self.copy(b).wait_recv()
-
-                    @pl.when(self.place < tp_size - 1)
-                    def _(b=b):
-                        grown = self.dst[b].astype(f32) * r.et[b][chunks : chunks + 1]
-                        self.src[b] = (grown + r.fresh[b]).astype(bf16)
-                        self.copy(b).start()
-
-        def end(self):
-            @pl.when(self.place < tp_size - 1)
-            def _():
-                for b in range(BLOCKS):
-                    self.copy(b).wait_send()
-
-    at_first, at_last = tp == 0, tp == tp_size - 1
-    s_chain = Chain(r.s_out, r.s_in, r.s_ss, r.s_rs, after, tp)
-    r_chain = Chain(r.r_out, r.r_in, r.r_ss, r.r_rs, before, tp_size - 1 - tp)
-    s_chain.begin()
+    s_chain.after_first()
 
     half = lax.broadcasted_iota(jnp.int32, (CHUNK, 128), 1) < 64
 
@@ -756,19 +782,13 @@
                 lanes, mixing, weights, split = pair_terms(b, c, i)
                 y[b, rows(c), lanes] = nn(weights, split)
 
-        loop(chunks, part)
-        s_chain.step(jnp.logical_and(b == 0, tp == 1))
+        loop(chunks, part, chunks)
+        s_chain.between(b)
 
     loop(BLOCKS, inside)
     if direct:
-        late.from_core()
-
-    def back_out(b):
-        gy[b] = small[b, 5:6, :] * (nn(gbr[...], wout[b]) + nn(ghid[...], r.odn[b]))
-
-    loop(BLOCKS, back_out)
-    for k in range(2, tp_size):
-        s_chain.step(tp == k)
+        late.from_x()
+    s_chain.rest()
 
     ssq, crs = r.ssq, r.crs
     ssq[...] = jnp.zeros_like(ssq)
@@ -784,14 +804,24 @@
             added = st[c, b]
             st[c, b] = state
             grown = nn(cb[rows(c), :], state.astype(bf16))
-            y[b, rows(c), :] = y[b, rows(c), :] + nn(ech[rows(c), :], expand[b]) * grown
+            y[b, rows(c), :] = y[b, rows(c), :] + nn(r.rates[c, 0:CHUNK, :], expand[b]) * grown
             state = r.et[b, c : c + 1, :] * state + added
             _, act = gated(b, c)
             ssq[rows(c), :] = ssq[rows(c), :] + thirds(act * act)
-            crs[rows(c), :] = crs[rows(c), :] + thirds(act * gy[b, rows(c), :])
         st[chunks, b] = state
 
     loop(BLOCKS, carried)
+    if direct:
+        late.from_core()
+
+    def back_out(b):
+        back = small[b, 5:6, :] * (nn(gbr[...], wout[b]) + nn(ghid[...], r.odn[b]))
+        gy[b] = back
+        for c in range(chunks):
+            _, act = gated(b, c)
+            crs[rows(c), :] = crs[rows(c), :] + thirds(act * back[c * CHUNK : (c + 1) * CHUNK])
+
+    loop(BLOCKS, back_out)
     inner = BLOCKS * WIDE
 
     def settle(c):
@@ -802,7 +832,7 @@
 
     loop(chunks, settle)
 
-    acc, nout, hout, hout_t = r.acc, r.nout, r.hout, r.hout_t
+    acc, nout, hout = r.acc, r.nout, r.hout
 
     def out_block(b):
         def part(c):
@@ -813,33 +843,31 @@
             g_y = g_gated * gate[b, rows(c), :]
             gy[b, rows(c), :] = g_y
             gzx[b, rows(c), :WIDE] = (g_gated * full * spz[b, rows(c), :].astype(f32)).astype(bf16)
-            rt[c, b] = nn(ct[c], (nn(ech[rows(c), :], expand[b]) * g_y).astype(bf16))
-
-        loop(chunks, part)
+            rt[c, b] = nn(ct[c], (nn(r.rates[c, 0:CHUNK, :], expand[b]) * g_y).astype(bf16))
+
+        loop(chunks, part, chunks)
         et = r.et[b]
         total = rt[chunks - 1, b]
         for c in range(chunks - 2, -1, -1):
             total = total * et[c : c + 1] + rt[c, b]
         r.fresh[b] = total
-        r.odg[b] = nn(r.ghid_t[...], nout[...])
+        r_chain.within(b)
+        r.odg[b] = tn(ghid[...], nout[...])
         part_b = nt(nout[...], wout[b])
         part_h = nt(nout[...], r.odn[b])
-        part_t = nt(r.odn[b], nout[...])
 
         @pl.when(b == 0)
         def _():
             acc[...] = part_b
             hout[...] = part_h
-            hout_t[...] = part_t
 
         @pl.when(b > 0)
         def _():
             acc[...] = acc[...] + part_b
             hout[...] = hout[...] + part_h
-            hout_t[...] = hout_t[...] + part_t
 
     loop(BLOCKS, out_block)
-    r_chain.begin()
+    r_chain.after_first()
 
     def write_out(c):
         branch = acc[rows(c), :] + nn(hout[rows(c), :].astype(bf16), r.oup[...])
@@ -847,8 +875,7 @@
         r.out_rows[rows(c), :] = (u + valid(c) * branch).astype(bf16)
 
     loop(chunks, write_out)
-    oug = nn(hout_t[...].astype(bf16), gbr[...])
-    r_chain.step(r_chain.place == 1)
+    oug = tn(hout[...].astype(bf16), gbr[...])
     if direct:
         write_back = pltpu.make_async_copy(r.out_rows, r.out, r.own_sem.at[5])
         write_back.start()
@@ -865,10 +892,10 @@
     dsc = r.dsc
     dsc[...] = jnp.zeros_like(dsc)
 
-    def inside_back(b):
-        turn_heads(b)
-
-        def part(c):
+    def inside_back(b, part):
+        for c in part:
+            r.cub[rows(c), :] = pltpu.roll(cu[rows(c), :], lax.rem(128 - SLOT * b, 128), 1)
+        for c in part:
             total = dsc[c]
             for i in range(HEADS_B // 2):
                 lanes, mixing, weights, split = pair_terms(b, c, i)
@@ -879,19 +906,16 @@
                 xp[b, rows(c), lanes] = jnp.where(half, back[:CHUNK], back[CHUNK:])
             dsc[c] = total
 
-        loop(chunks, part)
-        r_chain.step(jnp.logical_and(b == 2, r_chain.place == 2))
-        if direct:
-
-            @pl.when(b == 1)
-            def _():
-                rest.middle()
-
-    loop(BLOCKS, inside_back)
-    for k in range(3, tp_size):
-        r_chain.step(r_chain.place == k)
+    upper, lower = range(chunks // 2, chunks), range(chunks // 2)
+
+    def first_back(b):
+        inside_back(b, upper)
+        r_chain.between(b)
+
+    loop(BLOCKS, first_back)
+    r_chain.rest()
     if direct:
-        rest.gathered()
+        rest.middle()
 
     h1, h2, db, dc = r.h1, r.h2, r.db, r.dc
     for ref in (h1, h2, db, dc):
@@ -904,24 +928,29 @@
         sel = expand[b, :CHUNK, :]
         return nt(parts[:, :WIDE], sel) + nt(parts[:, WIDE:], sel)
 
-    def carried_back(b, part):
-        for c in part:
-            state = (r.r_in[b].astype(f32) if c == chunks - 1 else r.fresh[b])
-            low = state.astype(bf16)
-            meet = jnp.broadcast_to(jnp.sum(state * st[c + 1, b], axis=0, keepdims=True), (8, WIDE))
-            hs[c] = hs[c] + head_sum(meet, b)
-            tail = nn(tlh[rows(c), :], expand[b])
-            grow = nn(ech[rows(c), :], expand[b])
-            dt = nn(dth[rows(c), :], expand[b])
-            x, g = xs[b, rows(c), :], gy[b, rows(c), :]
-            back = xp[b, rows(c), :] + tail * nn(bb[rows(c), :], low)
-            xdt = x * dt
-            h1[rows(c), :] = h1[rows(c), :] + head_sum(g * y[b, rows(c), :] - xdt * back, b)
-            h2[rows(c), :] = h2[rows(c), :] + head_sum(x * back, b)
-            dc[rows(c), :] = dc[rows(c), :] + nt((grow * g).astype(bf16), st[c, b].astype(bf16))
-            db[rows(c), :] = db[rows(c), :] + nt((tail * xdt).astype(bf16), low)
-            px[b, rows(c), :] = (dt * back + r.skips[b, 8:9, :] * g) * spx[b, rows(c), :].astype(f32)
-            r.fresh[b] = r.et[b, c : c + 1, :] * state + rt[c, b]
+    def states_back(b):
+        state = r.r_in[b].astype(f32)
+        for c in range(chunks - 1, -1, -1):
+            added = rt[c, b]
+            rt[c, b] = state
+            state = r.et[b, c : c + 1, :] * state + added
+
+    loop(BLOCKS, states_back)
+
+    def carried_back(b, c):
+        state = rt[c, b]
+        low = state.astype(bf16)
+        meet = jnp.broadcast_to(jnp.sum(state * st[c + 1, b], axis=0, keepdims=True), (8, WIDE))
+        hs[c] = hs[c] + head_sum(meet, b)
+        wide = nn(r.rates[c], expand[b])
+        grow, dt, tail = wide[:CHUNK], wide[CHUNK : 2 * CHUNK], wide[2 * CHUNK :]
+        x, g = xs[b, rows(c), :], gy[b, rows(c), :]
+        back = xp[b, rows(c), :] + tail * nn(bb[rows(c), :], low)
+        h1[rows(c), :] = h1[rows(c), :] + head_sum(g * y[b, rows(c), :], b)
+        h2[rows(c), :] = h2[rows(c), :] + head_sum(x * back, b)
+        dc[rows(c), :] = dc[rows(c), :] + nt((grow * g).astype(bf16), st[c, b].astype(bf16))
+        db[rows(c), :] = db[rows(c), :] + nt((tail * x * dt).astype(bf16), low)
+        px[b, rows(c), :] = (dt * back + r.skips[b, 8:9, :] * g) * spx[b, rows(c), :].astype(f32)
 
     up_tri = jnp.where(
         lax.broadcasted_iota(jnp.int32, (CHUNK, CHUNK), 0) <= lax.broadcasted_iota(jnp.int32, (CHUNK, CHUNK), 1),
@@ -937,7 +966,9 @@
         u = ub[rows(c), :]
         s = sigmoid(u)
         pb[rows(c), :] = jnp.concatenate([d_b, d_c], axis=1) * (s + u * s * (1.0 - s))
-        da = jnp.dot(up_tri, h1[rows(c), :], precision=HIGHEST, preferred_element_type=f32) + hs[c, 0:1, :]
+        dt = r.rates[c, CHUNK : 2 * CHUNK, :128].astype(f32) + r.rates[c, CHUNK : 2 * CHUNK, 128:].astype(f32)
+        dcum = h1[rows(c), :] - dt * h2[rows(c), :]
+        da = jnp.dot(up_tri, dcum, precision=HIGHEST, preferred_element_type=f32) + hs[c, 0:1, :]
         gdt[rows(c), :] = ((h2[rows(c), :] + decay * da) * sigmoid(pd[rows(c), :])).astype(bf16)
 
     def edges():
@@ -981,77 +1012,89 @@
     if direct:
         returns = Returns(r, dp, tp, dp_size)
 
-    def finish_rows(at, size):
+    def conv_rows(at, size):
+        for b in range(BLOCKS):
+            window = px[b, at : at + size + 8, :]
+            g = conv_back(window, lambda j: small[b, j : j + 1, :]).astype(bf16)
+            gzx[b, at : at + size, WIDE:] = g
+        window = pb[at : at + size + 8, :]
+        r.gbc[at : at + size, :] = conv_back(window, lambda j: bc_kernel[j : j + 1, :]).astype(bf16)
+
+    def hidden_rows(at, size):
         here = slice(at, at + size)
-        gbc = conv_back(pb[at : at + size + 8, :], lambda j: bc_kernel[j : j + 1, :]).astype(bf16)
-        acc[here, :] = nt(gbc, r.wbc[...]) + nt(gdt[here, :], r.wdt[...])
-        hout[here, :] = jnp.zeros((size, 16), f32)
-
-        def in_block(b):
-            g = conv_back(px[b, at : at + size + 8, :], lambda j: small[b, j : j + 1, :]).astype(bf16)
-            gzx[b, here, WIDE:] = g
-            both = gzx[b, here, :]
-            acc[here, :] = acc[here, :] + nt(both, zx[b])
-            hout[here, :] = hout[here, :] + nt(both, up[b])
-
-        loop(BLOCKS, in_block)
-        g = acc[here, :] + nn(hout[here, :].astype(bf16), r.idn[...])
-        u = ext[at + HALO : at + HALO + size, :].astype(f32)
+        for b in range(BLOCKS):
+            part = nt(gzx[b, here, :], up[b])
+            hout[here, :] = part if b == 0 else hout[here, :] + part
+
+    def finish_rows(at, size, blocks=(), skip=0):
+        here = slice(at, at + size)
+        turned = nt(zx[0], gzx[0, here, :])
+        for b in range(1, BLOCKS):
+            turned = turned + nt(zx[b], gzx[b, here, :])
+        turned = turned + nt(r.wbc[...], r.gbc[here, :])
+        turned = turned + nt(r.wdt[...], gdt[here, :])
+        kept = slice(at + skip, at + size)
+        g = turned.T[skip:] + nn(hout[kept, :].astype(bf16), r.idn[...])
+        u = ext[at + skip + HALO : at + HALO + size, :].astype(f32)
         inv = lax.rsqrt(jnp.mean(u * u, axis=1, keepdims=True) + EPSILON)
         v = r.gain[...].astype(f32)[None] * g
         cross = jnp.mean(v * u, axis=1, keepdims=True)
-        r.tg[here, :] = (cot[here, :].astype(f32) + inv * v - u * (inv * inv * inv * cross)).astype(bf16)
+        r.tg[kept, :] = (cot[kept, :].astype(f32) + inv * v - u * (inv * inv * inv * cross)).astype(bf16)
         if direct:
-            for d in range(at // returns.block, (at + size) // returns.block):
+            for d in blocks:
                 returns.send(d)
 
-    upper = range(chunks - 1, chunks // 2 - 1, -1)
-    lower = range(chunks // 2 - 1, -1, -1)
-    loop(BLOCKS, lambda b: carried_back(b, upper))
+    block = r.tok_out.shape[1] if direct else CHUNK // 2
+    middle = rows_n // 2
+    loop(BLOCKS, lambda b: [carried_back(b, c) for c in upper])
     for c in upper:
         finish_bc(c)
-    middle = rows_n // 2
-    finish_rows(middle, middle - 64)
+    conv_rows(middle, middle - block)
+    hidden_rows(middle, middle - block)
     if direct:
-        rest.pass_on()
-    loop(BLOCKS, lambda b: carried_back(b, lower))
-    for c in lower:
+        finish_rows(middle, middle, range(middle // block, rows_n // block - 1))
+    per = CHUNK // block
+    for c in reversed(lower):
+        loop(BLOCKS, lambda b: inside_back(b, (c,)))
+        if direct and c == lower[-1]:
+            rest.gathered()
+        loop(BLOCKS, lambda b: carried_back(b, c), BLOCKS)
         finish_bc(c)
-    send_edges()
-    finish_rows(0, middle)
+        if c == 0:
+            send_edges()
+        conv_rows(c * CHUNK, CHUNK)
+        hidden_rows(c * CHUNK, CHUNK)
+        if direct and c == lower[-1]:
+            finish_rows(c * CHUNK, CHUNK, range(c * per, (c + 1) * per))
+            rest.pass_on()
     take_edges()
-    finish_rows(rows_n - 64, 64)
-
-    hid_t = nt(r.idn[...], nrm[HALO:, :]).astype(bf16)
-    ghin_t = hout_t
-    ghin_t[...] = jnp.zeros_like(ghin_t)
+    conv_rows(rows_n - block, block)
+    hidden_rows(rows_n - block, block)
 
     def adapter_grads(b):
-        g = gzx[b]
-        ghin_t[...] = ghin_t[...] + nt(up[b], g)
-        iug = nn(hid_t, g)
+        iug = tn(hid[HALO:, :], gzx[b])
         if direct:
             r.sum_out[0, b] = iug.astype(bf16)
         else:
             r.iug[b] = iug
 
-    loop(BLOCKS, adapter_grads)
-    idg = nn(ghin_t[...].astype(bf16), nrm[HALO:, :])
+    loop(BLOCKS, adapter_grads, BLOCKS)
+    idg = tn(hout[...].astype(bf16), nrm[HALO:, :])
+    if not direct:
+        for half in range(2):
+            finish_rows(half * middle, middle)
     if direct:
         ups = Sums(r, dp, tp, dp_size, tp_size, 0)
         ups.start()
-        ends = Toward(
-            tp,
-            tp_size,
-            lambda t: (dp, t),
-            lambda t: r.end_out,
-            lambda t: r.end_in.at[t],
-            r.ge_ss,
-            r.ge_rs,
-        )
-        r.end_out[...] = idg.astype(bf16)
+        to_tp = lambda t: (dp, t)
+        ends = Toward(tp, tp_size, to_tp, lambda t: r.end_out.at[t], lambda t: r.end_in.at[t], r.ge_ss, r.ge_rs)
+        low = idg.astype(bf16)
+        for t in range(3):
+            r.end_out[t] = low[:, t * 256 : (t + 1) * 256]
+        r.end_out[3] = jnp.zeros_like(r.end_out[3])
         ends.start()
-        r.end_in[tp] = r.end_out[...]
+        r.end_in[tp] = r.end_out[tp]
+        finish_rows(0, CHUNK)
         ups.middle()
         ends.wait()
         total = r.end_in[0].astype(f32)
@@ -1063,21 +1106,28 @@
             dp_size,
             lambda d: (d, tp),
             lambda d: r.end_all,
-            lambda d: r.all_end.at[d],
+            lambda d: r.all_end.at[tp, d],
             r.gf_ss,
             r.gf_rs,
         )
         spread.start()
-        own_end = pltpu.make_async_copy(r.end_all, r.all_end.at[dp], r.own_sem.at[6])
+        for d in range(per):
+            returns.send(d)
+        finish_rows(rows_n - CHUNK, CHUNK, [rows_n // block - 1], CHUNK - block)
+        own_end = pltpu.make_async_copy(r.end_all, r.all_end.at[tp, dp], r.own_sem.at[6])
         own_end.start()
-        ups.gathered()
         spread.wait()
         own_end.wait()
+        wide_end = Toward(tp, tp_size, to_tp, lambda t: r.all_end.at[tp], lambda t: r.all_end.at[t], r.gg_ss, r.gg_rs)
+        wide_end.start()
+        ups.gathered()
         returns.finish()
         rest.finish()
         ups.finish()
         ends.finish()
         spread.finish()
+        wide_end.wait()
+        wide_end.finish()
         write_back.wait()
         end_front()
     else:
@@ -1114,7 +1164,9 @@
     half = 2 * WIDE
     for s in range(count):
         k, g = adapters[s], dealt[s]
-        s_idg[k] = s_idg[k] + v_ends[g].astype(f32)
+        for i in range(3):
+            lanes = slice(256 * i, 256 * (i + 1))
+            s_idg[k, :, lanes] = s_idg[k, :, lanes] + v_ends[i, g].astype(f32)
         for i in range(2):
             s_iug[k, :, i, :] = s_iug[k, :, i, :] + v_ups[g, :, i * WIDE : (i + 1) * WIDE].astype(f32)
             s_odg[k, :, i * half : (i + 1) * half] = s_odg[k, :, i * half : (i + 1) * half] + v_rest[i, g].astype(f32)
@@ -1171,7 +1223,6 @@
         expand=((BLOCKS, 256, WIDE), bf16),
         skip=((16, 256), bf16),
         decay=((8, 128), f32),
-        ghid_t=((16, rows_n), bf16),
         skips=((BLOCKS, 16, WIDE), f32),
         nrm=((rows_n + HALO, d), bf16),
         hid=((rows_n + HALO, 16), bf16),
@@ -1183,9 +1234,7 @@
         xd=(wide, bf16),
         pb=((rows_n + HALO, 256), f32),
         pd=((rows_n, 128), f32),
-        dth=((rows_n, 256), bf16),
-        ech=((rows_n, 256), bf16),
-        tlh=((rows_n, 256), bf16),
+        rates=((chunks, 3 * CHUNK, 256), bf16),
         eth=((16, 256), bf16),
         et=((BLOCKS, 16, WIDE), f32),
         cu=((rows_n, 128), f32),
@@ -1215,7 +1264,6 @@
         acc=((rows_n, d), f32),
         nout=((rows_n, WIDE), bf16),
         hout=((rows_n, 16), f32),
-        hout_t=((16, rows_n), f32),
         dsc=((chunks, 128, 128), f32),
         h1=((rows_n, 128), f32),
         h2=((rows_n, 128), f32),
@@ -1223,6 +1271,7 @@
         dc=((rows_n, 128), f32),
         hs=((chunks, 8, 128), f32),
         gdt=((rows_n, 128), bf16),
+        gbc=((rows_n, 256), bf16),
         ex_out=((BLOCKS, 8, WIDE), f32),
         ex_in=((BLOCKS, 8, WIDE), f32),
         eb_out=((8, 256), f32),
@@ -1236,7 +1285,7 @@
             tg_in=((n, block, d), bf16),
             all_up=((n, 16, d), bf16),
             all_rest=((BLOCKS, n, 16, d), bf16),
-            all_end=((n, 16, d), bf16),
+            all_end=((BLOCKS, n, 16, 256), bf16),
         )
         scratch.update(
             out_rows=((rows_n, d), bf16),
@@ -1252,15 +1301,15 @@
             sum_out=((2, BLOCKS, 16, d), bf16),
             sum_in=((2, BLOCKS, 16, d), bf16),
             sum_all=((2, 16, d), bf16),
-            end_out=((16, d), bf16),
-            end_in=((BLOCKS, 16, d), bf16),
-            end_all=((16, d), bf16),
+            end_out=((BLOCKS, 16, 256), bf16),
+            end_in=((BLOCKS, 16, 256), bf16),
+            end_all=((16, 256), bf16),
         )
         for name in LOADED:
             scratch["v_" + name] = (arrays[name].shape, arrays[name].dtype)
         pairs = dict(zx=(6, n), wo=(6, n), bc=(3, n), tok=(n,), dt=(n,), d2=(BLOCKS,), up=(BLOCKS,), sm=(BLOCKS,))
         pairs.update(ha=(1,), tg=(n,), ga=(BLOCKS,), gb=(BLOCKS,), gc=(n,), gd=(n,), g3=(BLOCKS,))
-        pairs.update(ge=(BLOCKS,), gf=(n,))
+        pairs.update(ge=(BLOCKS,), gf=(n,), gg=(BLOCKS,))
         for name, shape in pairs.items():
             sems[name + "_ss"] = shape
             sems[name + "_rs"] = (BLOCKS, n) if name in ("zx", "wo") else shape[-1:]

time: 155 us -> 136 us (0.88); the launches traced: 155 us -> 135 us
  Pallas kernels: 154 us -> 134 us
    pallas_call x1, Pallas kernels: 150 us -> 130 us  [mixer_call(): pl.pallas_call(partial(mixer_kernel, direct, names), out_shape=[jax.Shape...]
where the time goes in v2:
time: 136 us; the launch traced here: 135 us
  Pallas kernels  134 us (99%)
    pallas_call x1, Pallas kernels, mixer_call(): pl.pallas_call(partial(mixer_kernel, direct, names), out_shape=[jax.Shape...  130 us
    pallas_call x1, Pallas kernels, settle_call(): pl.pallas_call(settle_kernel, out_shape=[jax.ShapeDtypeStruct(res.out.sha...  4.15 us

profile of v2, /device:TPU:0, one launch (start us, length us, event | category | flops | bytes accessed | tf_op | source)
XLA Modules:
  0.0 134.6 jit_solution(2279617920365407280)
XLA Ops:
  0.6 129.6 %shard_map.253 = (bf16[512,768]{1,0:T(8,128)(2,1)}, bf16[8,64,768]{2,1,0:T(8,128)(2,1)}, bf16[8,16,768]{2,1,0:T(8,128)(2,1)}, bf16[4,8,16,768]{3,2,1,0:T(8,128)(2,1)}, bf16[4,8,16,256]{3,2,1,0:T(8,128)(2,1)}) custom-call(s32[8]{0:T(128)} %refs_0_.1, s32[8]{0:T(128)} %dealt.1, s32[8]{0:T(128)} %adapters.1, bf16[8,64,768]{2,1,0:T(8,128)(2,1)} %bitcast.12, ...), custom_call_target="tpu_custom_call" | custom-call | tf_op jit(solution)/shard_map/pallas_call | solution.py:1320
  130.3 4.1 %shard_map.254 = (bf16[512,768]{1,0:T(8,128)(2,1)}, bf16[8,64,768]{2,1,0:T(8,128)(2,1)}, f32[8,16,768]{2,1,0:T(8,128)}, f32[8,16,2,384]{3,2,1,0:T(2,128)}, f32[8...) custom-call(s32[8]{0:T(128)} %dealt.1, s32[8]{0:T(128)} %adapters.1, bf16[512,768]{1,0:T(8,128)(2,1)} %get-tuple-element.17.out, ...), custom_call_target="tpu_custom_call" | custom-call | tf_op jit(solution)/shard_map/pallas_call | solution.py:1191
